TPU v7x, 32 devices: a whole 2x2x4 slice. The times are simulated.
32 devices in a mesh: member: 8 (over z, core), basin: 4 (over y, x).
Axes of the slice: x: 2, y: 2, z: 4, core: 2. Of those that a mesh axis runs over, the one named last changes fastest.
Arguments:
- prior_params: float32 [256, 8, 512], P('member', None, 'basin'), may hold values from -3 to 3
- lateral_flow: float32 [256, 2, 65536], P('member', None, 'basin'), may hold values from 0.2 to 2
- inflow_start: float32 [65536], P('basin'), may hold values from 0.5 to 4
- outflow_start: float32 [65536], P('basin'), may hold values from 0.5 to 4
- reach_count: int32 [512], P('basin'), may hold values from 64 to 128
- downstream: int32 [512], P('basin'), may hold values from 0 to 63
- gauge_reach: int32 [2048], P('basin'), may hold values from 0 to 16383
- observed: float32 [2, 2048], P(None, 'basin'), may hold values from 0.5 to 4
- obs_var: float32 [2, 2048], P(None, 'basin'), may hold values from 0.02 to 0.5
- obs_noise: float32 [256, 2, 2048], P('member', None, 'basin'), may hold values from -4 to 4
Outputs:
- posterior: float32 [256, 8, 512], P('member', None, 'basin')
- predicted: float32 [256, 2, 2048], P('member', None, 'basin')
All inputs are finite; a program needn't handle non-finite values.
Results may differ from a plain program's by a relative error of at most 0.0003.
Values sent between devices are 32-bit elements; how exact they have to be, the bound alone decides.
A program may use at most 128 MiB of HBM per device.

v0:
```python
import math

import jax
import jax.numpy as jnp
from jax import lax
from jax.sharding import PartitionSpec as P

LANES = 128
BLK_LEV = 64


exact_mode = lax.Precision.HIGHEST


def shifted(block, axis, distance):
    devices = range(lax.axis_size(axis))
    route = [(i - distance, i) for i in devices if i - distance in devices]
    return lax.ppermute(block, axis, route)


def inverse_sinh(values):
    return jnp.log(values + jnp.sqrt(values * values + 1.0))


def route_coefficients(prior_params):
    storage = 0.02 + 0.1 * jax.nn.sigmoid(prior_params[:, 0, :])
    weighting = 0.2 * jax.nn.sigmoid(prior_params[:, 1, :])
    denominator = storage * (1.0 - weighting) + 0.5
    weight_now = (0.5 - storage * weighting) / denominator
    weight_back = (0.5 + storage * weighting) / denominator
    weight_carry = (storage * (1.0 - weighting) - 0.5) / denominator
    return (weight_now[:, :, None], weight_back[:, :, None], weight_carry[:, :, None])


def lateral_scaling(prior_params, lane_count):
    lane_pos = jnp.arange(lane_count, dtype=jnp.float32)
    orders = jnp.arange(6, dtype=jnp.float32)
    cosine_modes = jnp.cos(math.pi * orders[:, None] * (lane_pos[None, :] + 0.5) / lane_count)
    exponent = jnp.einsum(
        "mkb,kr->mbr", 0.2 * prior_params[:, 2:, :], cosine_modes, precision=exact_mode
    )
    return jnp.exp(exponent)


def solve_gram(gram_matrix, cross_matrix):
    factor = jnp.linalg.cholesky(gram_matrix)
    halfway = lax.linalg.triangular_solve(factor, cross_matrix, left_side=True, lower=True)
    return lax.linalg.triangular_solve(
        factor, halfway, left_side=True, lower=True, transpose_a=True
    )


def level_sweep(incoming, weights, lateral_now, live_mask, one_hot, prev_in, prev_out):
    weight_now, weight_back, weight_carry, scaling = weights
    level_blocks = one_hot[0].shape[0]
    upstream = incoming
    inflows = []
    outflows = []
    for level_idx in range(len(one_hot)):
        level_span = slice(level_idx * level_blocks, (level_idx + 1) * level_blocks)
        inflow = live_mask[level_span] * (
            lateral_now[:, level_span] * scaling[:, level_span] + upstream
        )
        outflow = (
            weight_now[:, level_span] * inflow
            + weight_back[:, level_span] * prev_in[:, level_span]
            + weight_carry[:, level_span] * prev_out[:, level_span]
        )
        upstream = jnp.einsum("nj,gjr->gnr", one_hot[level_idx], outflow, precision=exact_mode)
        inflows.append(inflow)
        outflows.append(outflow)
    return (jnp.concatenate(inflows, 1), jnp.concatenate(outflows, 1), upstream)


def route_hour(mover, groups, weights, lateral_now, live_mask, one_hot, prev_in, prev_out):
    members_dev, block_dev, lane_count = prev_in.shape
    level_blocks = one_hot[0].shape[0]
    group_size = members_dev // groups
    basins = lax.axis_size("basin")
    basin_idx = lax.axis_index("basin")

    def advance(step_idx, state_tuple):
        incoming, inflow_all, outflow_all = state_tuple
        group_idx = step_idx - basin_idx
        active = (group_idx >= 0) & (group_idx < groups)
        first_row = jnp.clip(group_idx, 0, groups - 1) * group_size

        def compute(operands):
            arriving, inflow_keep, outflow_keep = operands

            def take_group(values):
                return lax.dynamic_slice_in_dim(values, first_row, group_size, 0)

            group_weights = tuple((take_group(item) for item in weights))
            inflow, outflow, passed = level_sweep(
                arriving,
                group_weights,
                take_group(lateral_now),
                live_mask,
                one_hot,
                take_group(prev_in),
                take_group(prev_out),
            )
            inflow_keep = lax.dynamic_update_slice_in_dim(inflow_keep, inflow, first_row, 0)
            outflow_keep = lax.dynamic_update_slice_in_dim(outflow_keep, outflow, first_row, 0)
            return (passed, inflow_keep, outflow_keep)

        def skipped(operands):
            return (jnp.zeros_like(operands[0]), operands[1], operands[2])

        passed, inflow_all, outflow_all = lax.cond(
            active, compute, skipped, (incoming, inflow_all, outflow_all)
        )
        return (mover(passed), inflow_all, outflow_all)

    initial = (
        jnp.zeros((group_size, level_blocks, lane_count), jnp.float32),
        jnp.zeros_like(prev_in),
        jnp.zeros_like(prev_out),
    )
    _, inflow_all, outflow_all = lax.fori_loop(0, basins + groups - 1, advance, initial)
    return (inflow_all, outflow_all)


def shards(
    prior_params,
    lateral_flow,
    inflow_start,
    outflow_start,
    reach_count,
    downstream,
    gauge_reach,
    observed,
    obs_var,
    obs_noise,
):
    members_dev, param_count, block_dev = prior_params.shape
    lane_count = LANES
    level_blocks = BLK_LEV
    level_count = block_dev // level_blocks
    hour_count = lateral_flow.shape[1]
    lane_ids = jnp.arange(lane_count, dtype=jnp.int32)
    live_mask = (lane_ids[None, :] < reach_count[:, None]).astype(jnp.float32)
    targets = jnp.arange(level_blocks, dtype=jnp.int32)
    one_hot = [
        (
            downstream[None, level_idx * level_blocks : (level_idx + 1) * level_blocks]
            == targets[:, None]
        ).astype(jnp.float32)
        for level_idx in range(level_count)
    ]
    weight_now, weight_back, weight_carry = route_coefficients(prior_params)
    scaling = lateral_scaling(prior_params, lane_count)
    weights = (weight_now, weight_back, weight_carry, scaling)
    lateral_grid = lateral_flow.reshape(members_dev, hour_count, block_dev, lane_count)
    prev_in = jnp.broadcast_to(
        (inflow_start.reshape(block_dev, lane_count) * live_mask)[None],
        (members_dev, block_dev, lane_count),
    )
    prev_out = jnp.broadcast_to(
        (outflow_start.reshape(block_dev, lane_count) * live_mask)[None],
        (members_dev, block_dev, lane_count),
    )
    results = []
    for hour_idx in range(hour_count):
        lateral_now = lateral_grid[:, hour_idx]
        prev_in, prev_out = route_hour(
            lambda passed: shifted(passed, "basin", 1),
            4,
            weights,
            lateral_now,
            live_mask,
            one_hot,
            prev_in,
            prev_out,
        )
        flat = prev_out.reshape(members_dev, block_dev * lane_count)
        results.append(inverse_sinh(jnp.take(flat, gauge_reach, axis=1)))
    predicted = jnp.stack(results, 1)
    members = members_dev * lax.axis_size("member")
    spread = jnp.sqrt(obs_var)
    spread_root = math.sqrt(members - 1.0)
    innovation = (observed + 2.0 * spread * obs_noise - predicted) / (2.0 * spread)
    mean_pred = lax.psum(jnp.sum(predicted, 0), "member") / members
    scaled = (predicted - mean_pred) / (spread_root * (2.0 * spread))
    scaled_all, innov_all = (
        lax.all_gather(scaled, "member", axis=0, tiled=True),
        lax.all_gather(innovation, "member", axis=0, tiled=True),
    )
    scaled_rows = scaled_all.reshape(members, -1)
    innov_rows = innov_all.reshape(members, -1)
    gram_part = jnp.dot(
        scaled_rows, scaled_rows.T, precision=exact_mode, preferred_element_type=jnp.float32
    )
    cross_part = jnp.dot(
        scaled_rows, innov_rows.T, precision=exact_mode, preferred_element_type=jnp.float32
    )
    gram_matrix, cross_matrix = lax.psum((gram_part, cross_part), "basin")
    gram_matrix = gram_matrix + jnp.eye(members, dtype=jnp.float32)
    solved = solve_gram(gram_matrix, cross_matrix)
    prior_all = lax.all_gather(prior_params, "member", axis=0, tiled=True)
    mean_prior = jnp.sum(prior_all, 0) / members
    anomaly = (prior_all - mean_prior) / spread_root
    own_cols = lax.dynamic_slice_in_dim(
        solved, lax.axis_index("member") * members_dev, members_dev, 1
    )
    posterior = prior_params + jnp.einsum("mn,mkb->nkb", own_cols, anomaly, precision=exact_mode)
    return (posterior, predicted)


def solution(mesh):
    return jax.shard_map(
        shards,
        mesh=mesh,
        in_specs=(
            P("member", None, "basin"),
            P("member", None, "basin"),
            P("basin"),
            P("basin"),
            P("basin"),
            P("basin"),
            P("basin"),
            P(None, "basin"),
            P(None, "basin"),
            P("member", None, "basin"),
        ),
        out_specs=(P("member", None, "basin"), P("member", None, "basin")),
        check_vma=False,
    )
```

profile of v0, /device:TPU:0, one launch (start us, length us, event | category | flops | bytes accessed | tf_op | source)
XLA Modules:
  0.0 468.4 jit_solution(3943242846933802712)
XLA Ops:
  12.6 6.6 %reshape.277 = f32[32,2,128,128]{3,2,1,0:T(8,128)} reshape(f32[32,2,16384]{2,1,0:T(2,128)} %param.21) | data formatting | bytes 8388608 | tf_op jit(solution)/shard_map/reshape | solution.py:155
  19.2 4.9 %slice_bitcast_fusion.13 = (f32[32,128,128]{2,1,0:T(8,128)}, f32[32,128,128]{2,1,0:T(8,128)}) fusion(f32[32,2,128,128]{3,2,1,0:T(8,128)} %reshape.277), kind=kLoop, calls=%fused_computation.78 | loop fusion | bytes 8388608 | tf_op jit(solution)/shard_map/squeeze | solution.py:166
  31.5 106.7 %while.39 = (s32[]{:T(128)}, f32[8,64,128]{2,1,0:T(8,128)S(1)}, f32[32,128,128]{2,1,0:T(8,128)}, f32[32,128,128]{2,1,0:T(8,128)}, s32[]{:T(128)}, /*index=5*/f32...) while((s32[]{:T(128)}, f32[8,64,128]{2,1,0:T(8,128)S(1)}, ...), condition=%wide.region_3.4_spmd.clone, body=%wide.region_0.3_spmd.clone.sunk | while | flops 102023184 | bytes 7075321 | solution.py:121
  33.0 5.8 %conditional.6 = (f32[8,64,128]{2,1,0:T(8,128)S(1)}, f32[32,128,128]{2,1,0:T(8,128)}, f32[32,128,128]{2,1,0:T(8,128)}) conditional(s32[]{:T(128)} %convert_element_type.73, (f32[32,128,128]{2,1,0:T(8,128)}, f32[32,128,128]{2,1,0:T(8,128)}) %tuple.149, (s32[]{:T(128)}, f32[32,128,1]{1,0,2:T(8,128)S(1)}, f32[128,128]{1,0:T(8,128)S(1)}, ...), branch_computations={%region_1.1_spmd, %region_2.2_spmd} | conditional | flops 101974024 | bytes 5927046 | solution.py:111
  40.1 6.5 %collective-permute-done = f32[8,64,128]{2,1,0:T(8,128)S(1)} collective-permute-done((f32[8,64,128]{2,1,0:T(8,128)S(1)}, f32[8,64,128]{2,1,0:T(8,128)S(1)}, u32[]{:S(2)}, u32[]{:S(2)}) %collective-permute-start) | collective-permute-done | bytes 262176 | tf_op jit(solution)/shard_map/while/body/eval_jaxpr/ppermute | solution.py:18
  47.9 5.7 %conditional.6 = (f32[8,64,128]{2,1,0:T(8,128)S(1)}, f32[32,128,128]{2,1,0:T(8,128)}, f32[32,128,128]{2,1,0:T(8,128)}) conditional(s32[]{:T(128)} %convert_element_type.73, (f32[32,128,128]{2,1,0:T(8,128)}, f32[32,128,128]{2,1,0:T(8,128)}) %tuple.149, (s32[]{:T(128)}, f32[32,128,1]{1,0,2:T(8,128)S(1)}, f32[128,128]{1,0:T(8,128)S(1)}, ...), branch_computations={%region_1.1_spmd, %region_2.2_spmd} | conditional | flops 101974024 | bytes 5927046 | solution.py:111
  58.1 5.6 %collective-permute-done = f32[8,64,128]{2,1,0:T(8,128)S(1)} collective-permute-done((f32[8,64,128]{2,1,0:T(8,128)S(1)}, f32[8,64,128]{2,1,0:T(8,128)S(1)}, u32[]{:S(2)}, u32[]{:S(2)}) %collective-permute-start) | collective-permute-done | bytes 262176 | tf_op jit(solution)/shard_map/while/body/eval_jaxpr/ppermute | solution.py:18
  65.2 5.8 %conditional.6 = (f32[8,64,128]{2,1,0:T(8,128)S(1)}, f32[32,128,128]{2,1,0:T(8,128)}, f32[32,128,128]{2,1,0:T(8,128)}) conditional(s32[]{:T(128)} %convert_element_type.73, (f32[32,128,128]{2,1,0:T(8,128)}, f32[32,128,128]{2,1,0:T(8,128)}) %tuple.149, (s32[]{:T(128)}, f32[32,128,1]{1,0,2:T(8,128)S(1)}, f32[128,128]{1,0:T(8,128)S(1)}, ...), branch_computations={%region_1.1_spmd, %region_2.2_spmd} | conditional | flops 101974024 | bytes 5927046 | solution.py:111
  81.5 5.8 %conditional.6 = (f32[8,64,128]{2,1,0:T(8,128)S(1)}, f32[32,128,128]{2,1,0:T(8,128)}, f32[32,128,128]{2,1,0:T(8,128)}) conditional(s32[]{:T(128)} %convert_element_type.73, (f32[32,128,128]{2,1,0:T(8,128)}, f32[32,128,128]{2,1,0:T(8,128)}) %tuple.149, (s32[]{:T(128)}, f32[32,128,1]{1,0,2:T(8,128)S(1)}, f32[128,128]{1,0:T(8,128)S(1)}, ...), branch_computations={%region_1.1_spmd, %region_2.2_spmd} | conditional | flops 101974024 | bytes 5927046 | solution.py:111
  97.1 10.3 %collective-permute-start = (f32[8,64,128]{2,1,0:T(8,128)S(1)}, f32[8,64,128]{2,1,0:T(8,128)S(1)}, u32[]{:S(2)}, u32[]{:S(2)}) collective-permute-start(f32[8,64,128]{2,1,0:T(8,128)S(1)} %get-tuple-element.1072), channel_id=1, source_target_pairs={{0,1},{1,2},{2,3},{4,5},{5,6},{6,7},{8,9},{9,10},{10,11},{12,13},{... | collective-permute-start | bytes 786440 | tf_op jit(solution)/shard_map/while/body/eval_jaxpr/ppermute | solution.py:18
  112.7 5.3 %collective-permute-start = (f32[8,64,128]{2,1,0:T(8,128)S(1)}, f32[8,64,128]{2,1,0:T(8,128)S(1)}, u32[]{:S(2)}, u32[]{:S(2)}) collective-permute-start(f32[8,64,128]{2,1,0:T(8,128)S(1)} %get-tuple-element.1072), channel_id=1, source_target_pairs={{0,1},{1,2},{2,3},{4,5},{5,6},{6,7},{8,9},{9,10},{10,11},{12,13},{... | collective-permute-start | bytes 786440 | tf_op jit(solution)/shard_map/while/body/eval_jaxpr/ppermute | solution.py:18
  123.4 11.0 %collective-permute-start = (f32[8,64,128]{2,1,0:T(8,128)S(1)}, f32[8,64,128]{2,1,0:T(8,128)S(1)}, u32[]{:S(2)}, u32[]{:S(2)}) collective-permute-start(f32[8,64,128]{2,1,0:T(8,128)S(1)} %get-tuple-element.1072), channel_id=1, source_target_pairs={{0,1},{1,2},{2,3},{4,5},{5,6},{6,7},{8,9},{9,10},{10,11},{12,13},{... | collective-permute-start | bytes 786440 | tf_op jit(solution)/shard_map/while/body/eval_jaxpr/ppermute | solution.py:18
  138.2 6.4 %copy.30 = f32[32,128,128]{0,2,1:T(8,128)} copy(f32[32,128,128]{2,1,0:T(8,128)} %get-tuple-element.1167) | data formatting | bytes 4194304 | tf_op jit(solution)/shard_map/while | solution.py:121
  146.2 98.9 %while.40 = (s32[]{:T(128)}, f32[8,64,128]{2,1,0:T(8,128)S(1)}, f32[32,128,128]{2,1,0:T(8,128)}, s32[]{:T(128)}, f32[32,128,1]{1,0,2:T(8,128)S(1)}, /*index=5*/f...) while((s32[]{:T(128)}, f32[8,64,128]{2,1,0:T(8,128)S(1)}, ...), condition=%wide.region_7.9_spmd.clone, body=%wide.region_4.8_spmd.clone.sunk | while | flops 101892112 | bytes 6157773 | solution.py:121
  147.7 5.1 %conditional.7 = (f32[8,64,128]{2,1,0:T(8,128)S(1)}, f32[32,128,128]{2,1,0:T(8,128)}) conditional(s32[]{:T(128)} %convert_element_type.76, f32[32,128,128]{2,1,0:T(8,128)} %get-tuple-element.1176, (s32[]{:T(128)}, f32[32,128,1]{1,0,2:T(8,128)S(1)}, f32[128,128]{1,0:T(8,128)S(1)}, f32[32,128,128]{2,1,0:T(8,128)}, f32[32,128,128]{2,1,0:T(8,128)S(1)}, ...), branch_computations={%region_5.6_spmd, %region_6.7_spmd} | conditional | flops 101842952 | bytes 5009530 | solution.py:111
  159.4 5.1 %conditional.7 = (f32[8,64,128]{2,1,0:T(8,128)S(1)}, f32[32,128,128]{2,1,0:T(8,128)}) conditional(s32[]{:T(128)} %convert_element_type.76, f32[32,128,128]{2,1,0:T(8,128)} %get-tuple-element.1176, (s32[]{:T(128)}, f32[32,128,1]{1,0,2:T(8,128)S(1)}, f32[128,128]{1,0:T(8,128)S(1)}, f32[32,128,128]{2,1,0:T(8,128)}, f32[32,128,128]{2,1,0:T(8,128)S(1)}, ...), branch_computations={%region_5.6_spmd, %region_6.7_spmd} | conditional | flops 101842952 | bytes 5009530 | solution.py:111
  164.5 5.7 %collective-permute-start.1 = (f32[8,64,128]{2,1,0:T(8,128)S(1)}, f32[8,64,128]{2,1,0:T(8,128)S(1)}, u32[]{:S(2)}, u32[]{:S(2)}) collective-permute-start(f32[8,64,128]{2,1,0:T(8,128)S(1)} %get-tuple-element.1091), channel_id=1, source_target_pairs={{0,1},{1,2},{2,3},{4,5},{5,6},{6,7},{8,9},{9,10},{10,11},{12,13},{... | collective-permute-start | bytes 786440 | tf_op jit(solution)/shard_map/while/body/eval_jaxpr/ppermute | solution.py:18
  175.5 5.1 %conditional.7 = (f32[8,64,128]{2,1,0:T(8,128)S(1)}, f32[32,128,128]{2,1,0:T(8,128)}) conditional(s32[]{:T(128)} %convert_element_type.76, f32[32,128,128]{2,1,0:T(8,128)} %get-tuple-element.1176, (s32[]{:T(128)}, f32[32,128,1]{1,0,2:T(8,128)S(1)}, f32[128,128]{1,0:T(8,128)S(1)}, f32[32,128,128]{2,1,0:T(8,128)}, f32[32,128,128]{2,1,0:T(8,128)S(1)}, ...), branch_computations={%region_5.6_spmd, %region_6.7_spmd} | conditional | flops 101842952 | bytes 5009530 | solution.py:111
  190.3 5.1 %conditional.7 = (f32[8,64,128]{2,1,0:T(8,128)S(1)}, f32[32,128,128]{2,1,0:T(8,128)}) conditional(s32[]{:T(128)} %convert_element_type.76, f32[32,128,128]{2,1,0:T(8,128)} %get-tuple-element.1176, (s32[]{:T(128)}, f32[32,128,1]{1,0,2:T(8,128)S(1)}, f32[128,128]{1,0:T(8,128)S(1)}, f32[32,128,128]{2,1,0:T(8,128)}, f32[32,128,128]{2,1,0:T(8,128)S(1)}, ...), branch_computations={%region_5.6_spmd, %region_6.7_spmd} | conditional | flops 101842952 | bytes 5009530 | solution.py:111
  205.2 9.5 %collective-permute-start.1 = (f32[8,64,128]{2,1,0:T(8,128)S(1)}, f32[8,64,128]{2,1,0:T(8,128)S(1)}, u32[]{:S(2)}, u32[]{:S(2)}) collective-permute-start(f32[8,64,128]{2,1,0:T(8,128)S(1)} %get-tuple-element.1091), channel_id=1, source_target_pairs={{0,1},{1,2},{2,3},{4,5},{5,6},{6,7},{8,9},{9,10},{10,11},{12,13},{... | collective-permute-start | bytes 786440 | tf_op jit(solution)/shard_map/while/body/eval_jaxpr/ppermute | solution.py:18
  214.7 5.5 %collective-permute-done.1 = f32[8,64,128]{2,1,0:T(8,128)S(1)} collective-permute-done((f32[8,64,128]{2,1,0:T(8,128)S(1)}, f32[8,64,128]{2,1,0:T(8,128)S(1)}, u32[]{:S(2)}, u32[]{:S(2)}) %collective-permute-start.1) | collective-permute-done | bytes 262176 | tf_op jit(solution)/shard_map/while/body/eval_jaxpr/ppermute | solution.py:18
  232.2 9.1 %collective-permute-start.1 = (f32[8,64,128]{2,1,0:T(8,128)S(1)}, f32[8,64,128]{2,1,0:T(8,128)S(1)}, u32[]{:S(2)}, u32[]{:S(2)}) collective-permute-start(f32[8,64,128]{2,1,0:T(8,128)S(1)} %get-tuple-element.1091), channel_id=1, source_target_pairs={{0,1},{1,2},{2,3},{4,5},{5,6},{6,7},{8,9},{9,10},{10,11},{12,13},{... | collective-permute-start | bytes 786440 | tf_op jit(solution)/shard_map/while/body/eval_jaxpr/ppermute | solution.py:18
  245.2 6.3 %copy.32 = f32[32,128,128]{0,2,1:T(8,128)} copy(f32[32,128,128]{2,1,0:T(8,128)} %get-tuple-element.648) | data formatting | bytes 4194304 | tf_op jit(solution)/shard_map/while | solution.py:121
  261.4 13.6 %psum.21 = f32[2,512]{1,0:T(2,128)S(1)} all-reduce(f32[2,512]{1,0:T(2,128)S(1)} %get-tuple-element.849), channel_id=1, replica_groups=mesh['member'=8,'basin'=4] {'member'}, use_global_device_ids=true, to_apply=%region_9.11 | all-reduce | flops 1024 | bytes 8192 | tf_op jit(solution)/shard_map/psum | solution.py:184
  277.4 23.8 %all-gather.4.cloned.1.call-done = f32[256,2,512]{2,0,1:T(8,128)} async-done(((f32[32,2,512]{2,0,1:T(8,128)}), f32[256,2,512]{2,0,1:T(8,128)}) %all-gather.4.cloned.1.call-update) | async-done | bytes 1048592 | tf_op jit(solution)/shard_map/all_gather | solution.py:187
  304.5 20.7 %all-gather.6.cloned.1.call-done = f32[256,2,512]{2,0,1:T(8,128)} async-done(((f32[32,2,512]{2,0,1:T(8,128)}), f32[256,2,512]{2,0,1:T(8,128)}) %all-gather.6.cloned.1.call-update) | async-done | bytes 1048592 | tf_op jit(solution)/shard_map/all_gather | solution.py:188
  329.0 19.7 %all-gather.8.cloned.1.call-done = f32[256,8,128]{2,1,0:T(8,128)} async-done(((f32[32,8,128]{2,1,0:T(8,128)}), f32[256,8,128]{2,1,0:T(8,128)}) %all-gather.8.cloned.1.call-update) | async-done | bytes 1048592 | tf_op jit(solution)/shard_map/all_gather | solution.py:201
  351.5 45.1 %all-reduce.4.cloned.1.call-done = (f32[256,256]{1,0:T(8,128)}, f32[256,256]{0,1:T(8,128)}) async-done(((f32[256,256]{1,0:T(8,128)}, f32[256,256]{0,1:T(8,128)}), (f32[256,256]{1,0:T(8,128)}, f32[256,256]{0,1:T(8,128)})) %all-reduce.4.cloned.1.call-update) | async-done | bytes 524304 | tf_op jit(solution)/shard_map/psum | solution.py:198
  398.7 11.7 %cholesky.49 = f32[128,128]{1,0:T(8,128)S(1)} custom-call(f32[128,128]{1,0:T(8,128)S(1)} %cholesky.115), custom_call_target="Cholesky" | custom-call | tf_op jit(solution)/shard_map/jit(cholesky)/cholesky | solution.py:46
  410.5 9.8 %custom-call.16 = f32[1,128,128]{1,2,0:T(8,128)S(1)} custom-call(f32[1,128,128]{2,1,0:T(8,128)S(1)} %get-tuple-element.857), custom_call_target="InvertDiagBlocksLowerTriangular" | custom-call | tf_op jit(solution)/shard_map/jit(cholesky)/cholesky | solution.py:46
  420.8 11.9 %cholesky.102 = f32[128,128]{1,0:T(8,128)S(1)} custom-call(f32[128,128]{1,0:T(8,128)S(1)} %convolution_subtract_fusion.2), custom_call_target="Cholesky" | custom-call | tf_op jit(solution)/shard_map/jit(cholesky)/cholesky | solution.py:46
  438.7 19.7 %custom-call.17 = f32[2,128,128]{1,2,0:T(8,128)S(1)} custom-call(f32[2,128,128]{2,1,0:T(8,128)S(1)} %get-tuple-element.656), custom_call_target="InvertDiagBlocksLowerTriangular" | custom-call | tf_op jit(solution)/shard_map/triangular_solve | solution.py:48
  (240 shorter events, 187.4 us)
Async XLA Ops:
  7.2 294.0 %all-gather.4.cloned.1.call-start = ((), (), s32[]{:S(2)}) async-start(), calls=%async_computation | async-start | bytes 1179648 | tf_op jit(solution)/shard_map/all_gather | solution.py:187
  19.2 4.9 %copy-start.1 = (f32[32,8,128]{2,1,0:T(8,128)S(1)}, f32[32,8,128]{2,1,0:T(8,128)}, u32[]{:S(2)}) copy-start(f32[32,8,128]{2,1,0:T(8,128)} %param.20) | copy-start | bytes 393220
  24.1 3.5 copy-start.5
  24.1 3.5 copy-start.6
  38.7 7.8 %collective-permute-start = (f32[8,64,128]{2,1,0:T(8,128)S(1)}, f32[8,64,128]{2,1,0:T(8,128)S(1)}, u32[]{:S(2)}, u32[]{:S(2)}) collective-permute-start(f32[8,64,128]{2,1,0:T(8,128)S(1)} %get-tuple-element.1072), channel_id=1, source_target_pairs={{0,1},{1,2},{2,3},{4,5},{5,6},{6,7},{8,9},{9,10},{10,11},{12,13},{... | collective-permute-start | bytes 786440 | tf_op jit(solution)/shard_map/while/body/eval_jaxpr/ppermute | solution.py:18
  53.7 10.0 %collective-permute-start = (f32[8,64,128]{2,1,0:T(8,128)S(1)}, f32[8,64,128]{2,1,0:T(8,128)S(1)}, u32[]{:S(2)}, u32[]{:S(2)}) collective-permute-start(f32[8,64,128]{2,1,0:T(8,128)S(1)} %get-tuple-element.1072), channel_id=1, source_target_pairs={{0,1},{1,2},{2,3},{4,5},{5,6},{6,7},{8,9},{9,10},{10,11},{12,13},{... | collective-permute-start | bytes 786440 | tf_op jit(solution)/shard_map/while/body/eval_jaxpr/ppermute | solution.py:18
  70.9 9.2 %collective-permute-start = (f32[8,64,128]{2,1,0:T(8,128)S(1)}, f32[8,64,128]{2,1,0:T(8,128)S(1)}, u32[]{:S(2)}, u32[]{:S(2)}) collective-permute-start(f32[8,64,128]{2,1,0:T(8,128)S(1)} %get-tuple-element.1072), channel_id=1, source_target_pairs={{0,1},{1,2},{2,3},{4,5},{5,6},{6,7},{8,9},{9,10},{10,11},{12,13},{... | collective-permute-start | bytes 786440 | tf_op jit(solution)/shard_map/while/body/eval_jaxpr/ppermute | solution.py:18
  87.3 8.3 %collective-permute-start = (f32[8,64,128]{2,1,0:T(8,128)S(1)}, f32[8,64,128]{2,1,0:T(8,128)S(1)}, u32[]{:S(2)}, u32[]{:S(2)}) collective-permute-start(f32[8,64,128]{2,1,0:T(8,128)S(1)} %get-tuple-element.1072), channel_id=1, source_target_pairs={{0,1},{1,2},{2,3},{4,5},{5,6},{6,7},{8,9},{9,10},{10,11},{12,13},{... | collective-permute-start | bytes 786440 | tf_op jit(solution)/shard_map/while/body/eval_jaxpr/ppermute | solution.py:18
  97.1 14.2 %collective-permute-start = (f32[8,64,128]{2,1,0:T(8,128)S(1)}, f32[8,64,128]{2,1,0:T(8,128)S(1)}, u32[]{:S(2)}, u32[]{:S(2)}) collective-permute-start(f32[8,64,128]{2,1,0:T(8,128)S(1)} %get-tuple-element.1072), channel_id=1, source_target_pairs={{0,1},{1,2},{2,3},{4,5},{5,6},{6,7},{8,9},{9,10},{10,11},{12,13},{... | collective-permute-start | bytes 786440 | tf_op jit(solution)/shard_map/while/body/eval_jaxpr/ppermute | solution.py:18
  112.7 9.1 %collective-permute-start = (f32[8,64,128]{2,1,0:T(8,128)S(1)}, f32[8,64,128]{2,1,0:T(8,128)S(1)}, u32[]{:S(2)}, u32[]{:S(2)}) collective-permute-start(f32[8,64,128]{2,1,0:T(8,128)S(1)} %get-tuple-element.1072), channel_id=1, source_target_pairs={{0,1},{1,2},{2,3},{4,5},{5,6},{6,7},{8,9},{9,10},{10,11},{12,13},{... | collective-permute-start | bytes 786440 | tf_op jit(solution)/shard_map/while/body/eval_jaxpr/ppermute | solution.py:18
  123.4 14.9 %collective-permute-start = (f32[8,64,128]{2,1,0:T(8,128)S(1)}, f32[8,64,128]{2,1,0:T(8,128)S(1)}, u32[]{:S(2)}, u32[]{:S(2)}) collective-permute-start(f32[8,64,128]{2,1,0:T(8,128)S(1)} %get-tuple-element.1072), channel_id=1, source_target_pairs={{0,1},{1,2},{2,3},{4,5},{5,6},{6,7},{8,9},{9,10},{10,11},{12,13},{... | collective-permute-start | bytes 786440 | tf_op jit(solution)/shard_map/while/body/eval_jaxpr/ppermute | solution.py:18
  152.8 5.2 %collective-permute-start.1 = (f32[8,64,128]{2,1,0:T(8,128)S(1)}, f32[8,64,128]{2,1,0:T(8,128)S(1)}, u32[]{:S(2)}, u32[]{:S(2)}) collective-permute-start(f32[8,64,128]{2,1,0:T(8,128)S(1)} %get-tuple-element.1091), channel_id=1, source_target_pairs={{0,1},{1,2},{2,3},{4,5},{5,6},{6,7},{8,9},{9,10},{10,11},{12,13},{... | collective-permute-start | bytes 786440 | tf_op jit(solution)/shard_map/while/body/eval_jaxpr/ppermute | solution.py:18
  164.5 9.5 %collective-permute-start.1 = (f32[8,64,128]{2,1,0:T(8,128)S(1)}, f32[8,64,128]{2,1,0:T(8,128)S(1)}, u32[]{:S(2)}, u32[]{:S(2)}) collective-permute-start(f32[8,64,128]{2,1,0:T(8,128)S(1)} %get-tuple-element.1091), channel_id=1, source_target_pairs={{0,1},{1,2},{2,3},{4,5},{5,6},{6,7},{8,9},{9,10},{10,11},{12,13},{... | collective-permute-start | bytes 786440 | tf_op jit(solution)/shard_map/while/body/eval_jaxpr/ppermute | solution.py:18
  180.6 8.3 %collective-permute-start.1 = (f32[8,64,128]{2,1,0:T(8,128)S(1)}, f32[8,64,128]{2,1,0:T(8,128)S(1)}, u32[]{:S(2)}, u32[]{:S(2)}) collective-permute-start(f32[8,64,128]{2,1,0:T(8,128)S(1)} %get-tuple-element.1091), channel_id=1, source_target_pairs={{0,1},{1,2},{2,3},{4,5},{5,6},{6,7},{8,9},{9,10},{10,11},{12,13},{... | collective-permute-start | bytes 786440 | tf_op jit(solution)/shard_map/while/body/eval_jaxpr/ppermute | solution.py:18
  195.5 8.3 %collective-permute-start.1 = (f32[8,64,128]{2,1,0:T(8,128)S(1)}, f32[8,64,128]{2,1,0:T(8,128)S(1)}, u32[]{:S(2)}, u32[]{:S(2)}) collective-permute-start(f32[8,64,128]{2,1,0:T(8,128)S(1)} %get-tuple-element.1091), channel_id=1, source_target_pairs={{0,1},{1,2},{2,3},{4,5},{5,6},{6,7},{8,9},{9,10},{10,11},{12,13},{... | collective-permute-start | bytes 786440 | tf_op jit(solution)/shard_map/while/body/eval_jaxpr/ppermute | solution.py:18
  205.2 15.0 %collective-permute-start.1 = (f32[8,64,128]{2,1,0:T(8,128)S(1)}, f32[8,64,128]{2,1,0:T(8,128)S(1)}, u32[]{:S(2)}, u32[]{:S(2)}) collective-permute-start(f32[8,64,128]{2,1,0:T(8,128)S(1)} %get-tuple-element.1091), channel_id=1, source_target_pairs={{0,1},{1,2},{2,3},{4,5},{5,6},{6,7},{8,9},{9,10},{10,11},{12,13},{... | collective-permute-start | bytes 786440 | tf_op jit(solution)/shard_map/while/body/eval_jaxpr/ppermute | solution.py:18
  221.7 9.1 %collective-permute-start.1 = (f32[8,64,128]{2,1,0:T(8,128)S(1)}, f32[8,64,128]{2,1,0:T(8,128)S(1)}, u32[]{:S(2)}, u32[]{:S(2)}) collective-permute-start(f32[8,64,128]{2,1,0:T(8,128)S(1)} %get-tuple-element.1091), channel_id=1, source_target_pairs={{0,1},{1,2},{2,3},{4,5},{5,6},{6,7},{8,9},{9,10},{10,11},{12,13},{... | collective-permute-start | bytes 786440 | tf_op jit(solution)/shard_map/while/body/eval_jaxpr/ppermute | solution.py:18
  232.2 12.9 %collective-permute-start.1 = (f32[8,64,128]{2,1,0:T(8,128)S(1)}, f32[8,64,128]{2,1,0:T(8,128)S(1)}, u32[]{:S(2)}, u32[]{:S(2)}) collective-permute-start(f32[8,64,128]{2,1,0:T(8,128)S(1)} %get-tuple-element.1091), channel_id=1, source_target_pairs={{0,1},{1,2},{2,3},{4,5},{5,6},{6,7},{8,9},{9,10},{10,11},{12,13},{... | collective-permute-start | bytes 786440 | tf_op jit(solution)/shard_map/while/body/eval_jaxpr/ppermute | solution.py:18
  245.2 6.3 %copy-start.7 = (s32[512]{0:T(512)S(1)}, s32[512]{0:T(512)}, u32[]{:S(2)}) copy-start(s32[512]{0:T(512)} %compare_select_fusion) | copy-start | bytes 6148
  245.2 15.4 %copy-start.9 = (f32[2,512]{1,0:T(2,128)S(1)}, f32[2,512]{1,0:T(2,128)}, u32[]{:S(2)}) copy-start(f32[2,512]{1,0:T(2,128)} %param.28) | copy-start | bytes 12292
  245.2 15.4 %copy-start.10 = (pred[512]{0:T(512)(128)(4,1)S(1)}, pred[512]{0:T(512)(128)(4,1)}, u32[]{:S(2)}) copy-start(pred[512]{0:T(512)(128)(4,1)} %compare_and_fusion) | copy-start | bytes 1540
  251.4 9.2 %copy-start.4 = (f32[32,2,512]{2,1,0:T(2,128)S(1)}, f32[32,2,512]{2,1,0:T(2,128)}, u32[]{:S(2)}) copy-start(f32[32,2,512]{2,1,0:T(2,128)} %param.29) | copy-start | bytes 393220
  251.4 9.2 %copy-start.8 = (f32[2,512]{1,0:T(2,128)S(1)}, f32[2,512]{1,0:T(2,128)}, u32[]{:S(2)}) copy-start(f32[2,512]{1,0:T(2,128)} %param.27) | copy-start | bytes 12292
  275.7 49.6 %all-gather.6.cloned.1.call-start = ((), (), s32[]{:S(2)}) async-start(), calls=%async_computation.1 | async-start | bytes 1179648 | tf_op jit(solution)/shard_map/all_gather | solution.py:188
  276.4 72.3 %all-gather.8.cloned.1.call-start = ((), (), s32[]{:S(2)}) async-start(), calls=%async_computation.2 | async-start | bytes 1179648 | tf_op jit(solution)/shard_map/all_gather | solution.py:201
  277.2 119.4 %all-reduce.4.cloned.1.call-start = ((), (), s32[]{:S(2)}) async-start(), calls=%async_computation.3 | async-start | bytes 1048576 | tf_op jit(solution)/shard_map/psum | solution.py:198
  301.2 24.1 %copy-start = (f32[256,2,512]{2,0,1:T(8,128)S(1)}, f32[256,2,512]{2,0,1:T(8,128)}, u32[]{:S(2)}) copy-start(f32[256,2,512]{2,0,1:T(8,128)} %all-gather.4.cloned.1.call-done) | copy-start | bytes 3145732
  397.6 60.8 %copy-start.3 = (f32[256,256]{1,0:T(8,128)S(1)}, f32[256,256]{1,0:T(8,128)}, u32[]{:S(2)}) copy-start(f32[256,256]{1,0:T(8,128)} %get-tuple-element.810) | copy-start | bytes 786436
  420.3 39.9 %copy-start.2 = (f32[32,8,128]{2,1,0:T(8,128)S(1)}, f32[32,8,128]{2,1,0:T(8,128)}, u32[]{:S(2)}) copy-start(f32[32,8,128]{2,1,0:T(8,128)} %param.20) | copy-start | bytes 393220
Sparse Core Ops, SparseCore 0:
  275.8 25.3 all-gather.3
  303.4 21.8 all-gather.5
  326.8 21.8 all-gather.7
  351.5 45.0 all-reduce.3
where the time goes:
time: 471 us; the launch traced here: 468 us
  waiting for transfers between devices  172 us (37%)
  other arithmetic  102 us (22%)
  starting transfers between devices  80.2 us (17%)
  local copies, waits for them, and re-layouts  56.3 us (12%)
  matrix products  27.6 us (6%)
  between operations  15.4 us (3%)
  blocking collectives  13.6 us (3%)
    ppermute x14, starting transfers between devices, shifted(): return lax.ppermute(block, axis, route)  79.8 us
    ppermute x14, waiting for transfers between devices, shifted(): return lax.ppermute(block, axis, route)  61.7 us
    psum x1, waiting for transfers between devices, shards(): gram_matrix, cross_matrix = lax.psum((gram_part, cross_part), 'basin')  45.1 us
    another operation x6, other arithmetic, solve_gram(): factor = jnp.linalg.cholesky(gram_matrix)  34.1 us
    all_gather x1, waiting for transfers between devices, shards(): lax.all_gather(scaled, 'member', axis=0, tiled=True)  23.8 us
    all_gather x1, waiting for transfers between devices, shards(): lax.all_gather(innovation, 'member', axis=0, tiled=True)  20.7 us
    another operation x3, other arithmetic, solve_gram(): lax.linalg.triangular_solve(factor, halfway, left_side=True, lower=True,...  19.7 us
    all_gather x1, waiting for transfers between devices, shards(): prior_all = lax.all_gather(prior_params, 'member', axis=0, tiled=True)  19.7 us
  transfers between devices with their start and end apart: 18, of which 18 were waited for; matrix products, arithmetic and copies ran while one was open for 2% of the time, Pallas kernels for 0%

commit v1 on v0

v1 whole, which is shorter than its diff:
```python
import functools
import math

import jax
import jax.numpy as jnp
from jax import lax
from jax.experimental import pallas as pl
from jax.experimental.pallas import tpu as pltpu
from jax.sharding import PartitionSpec as P

LANES = 128
BLK_LEV = 64
exact_mode = lax.Precision.HIGHEST
VMEM = pltpu.VMEM
SMEM = pltpu.SMEM
MESH = pl.DeviceIdType.MESH


def vmem_spec():
    return pl.BlockSpec(memory_space=VMEM)


def smem_spec():
    return pl.BlockSpec(memory_space=SMEM)


def exchange_body(axis, n, spread_out, x_ref, o_ref, send_sem, recv_sem, own_sem):
    me = lax.axis_index(axis)
    barrier = pltpu.get_barrier_semaphore()
    for i in range(1, n):
        pl.semaphore_signal(
            barrier, inc=1, device_id={axis: lax.rem(me + i, n)}, device_id_type=MESH
        )
    pl.semaphore_wait(barrier, n - 1)
    copies = []
    for i in range(1, n):
        peer = lax.rem(me + i, n)
        copies.append(
            pltpu.make_async_remote_copy(
                src_ref=x_ref.at[peer] if spread_out else x_ref,
                dst_ref=o_ref.at[me],
                send_sem=send_sem.at[i - 1],
                recv_sem=recv_sem.at[i - 1],
                device_id={axis: peer},
                device_id_type=MESH,
            )
        )
    for copy in copies:
        copy.start()
    own = pltpu.make_async_copy(x_ref.at[me] if spread_out else x_ref, o_ref.at[me], own_sem)
    own.start()
    own.wait()
    for copy in copies:
        copy.wait()


def exchange(x, axis, collective_id, spread_out=False):
    n = lax.axis_size(axis)
    shape = x.shape if spread_out else (n,) + x.shape
    return pl.pallas_call(
        functools.partial(exchange_body, axis, n, spread_out),
        out_shape=jax.ShapeDtypeStruct(shape, x.dtype),
        in_specs=[vmem_spec()],
        out_specs=vmem_spec(),
        scratch_shapes=[
            pltpu.SemaphoreType.DMA((n - 1,)),
            pltpu.SemaphoreType.DMA((n - 1,)),
            pltpu.SemaphoreType.DMA,
        ],
        compiler_params=pltpu.CompilerParams(collective_id=collective_id, has_side_effects=True),
        name=f"exchange_{collective_id}",
    )(x)


def doubling_bits(n):
    bits = []
    bit = n // 2
    while bit:
        bits.append(bit)
        bit //= 2
    return bits


def doubling_body(axis, n, x_ref, o_ref, send_sem, recv_sem, own_sem):
    me = lax.axis_index(axis)
    partners = [me + bit * (1 - 2 * lax.rem(me // bit, 2)) for bit in doubling_bits(n)]
    barrier = pltpu.get_barrier_semaphore()
    for partner in partners:
        pl.semaphore_signal(barrier, inc=1, device_id={axis: partner}, device_id_type=MESH)
    own = pltpu.make_async_copy(x_ref, o_ref.at[0], own_sem)
    own.start()
    own.wait()
    pl.semaphore_wait(barrier, len(partners))
    for k, partner in enumerate(partners):
        held = 2**k
        copy = pltpu.make_async_remote_copy(
            src_ref=o_ref.at[pl.ds(0, held)],
            dst_ref=o_ref.at[pl.ds(held, held)],
            send_sem=send_sem.at[k],
            recv_sem=recv_sem.at[k],
            device_id={axis: partner},
            device_id_type=MESH,
        )
        copy.start()
        copy.wait()


def doubling_gather(x, axis, collective_id):
    n = lax.axis_size(axis)
    steps = len(doubling_bits(n))
    return pl.pallas_call(
        functools.partial(doubling_body, axis, n),
        out_shape=jax.ShapeDtypeStruct((n,) + x.shape, x.dtype),
        in_specs=[vmem_spec()],
        out_specs=vmem_spec(),
        scratch_shapes=[
            pltpu.SemaphoreType.DMA((steps,)),
            pltpu.SemaphoreType.DMA((steps,)),
            pltpu.SemaphoreType.DMA,
        ],
        compiler_params=pltpu.CompilerParams(collective_id=collective_id, has_side_effects=True),
        name=f"doubling_{collective_id}",
    )(x)


def permuted_gather(x, axis):
    n = lax.axis_size(axis)
    held = x[None]
    for bit in doubling_bits(n):
        other = lax.ppermute(held, axis, [(i, i ^ bit) for i in range(n)])
        held = jnp.concatenate([held, other], 0)
    return held


def route_body(
    seg_count, level_count, members, gauges,
    basin_ref, down_ref, count_ref, gauge_ref,
    now_ref, back_ref, carry_ref, par_ref, cos_ref, lat_ref, pin_ref, pout_ref, pick_ref, fold_ref,
    out_ref,
    up_ref, flow_ref, row_ref,
):
    first = basin_ref[0]
    lev = BLK_LEV
    seg_blocks = level_count * lev
    rows = members
    shape = (rows, LANES)
    place = (lax.broadcasted_iota(jnp.int32, shape, 1) // members) * members
    place = place + lax.broadcasted_iota(jnp.int32, shape, 0)
    zero = jnp.zeros(shape, jnp.float32)

    def clear(i, _):
        up_ref[i] = jnp.zeros((2 * rows, LANES), jnp.float32)
        return 0

    def sweep(seg, level, parity, own):
        base = seg * seg_blocks + level * lev

        def block(j, _):
            b = base + j
            here = level * lev + j
            live = place < count_ref[b]
            now = now_ref[pl.ds(b, 1), :]
            back = back_ref[pl.ds(b, 1), :]
            carry = carry_ref[pl.ds(b, 1), :]
            if own:
                expo = cos_ref[0] * par_ref[0, pl.ds(here, 1), :]
                for k in range(1, cos_ref.shape[0]):
                    expo = expo + cos_ref[k] * par_ref[k, pl.ds(here, 1), :]
                scale = jnp.exp(expo)
                add0 = lat_ref[here, 0] * scale
                add1 = lat_ref[here, 1] * scale
                if level > 0:
                    add0 = add0 + up_ref[parity * lev + j, :rows]
                    add1 = add1 + up_ref[parity * lev + j, rows:]
                in0 = jnp.where(live, add0, 0.0)
                in1 = jnp.where(live, add1, 0.0)
                start = back * pin_ref[here] + carry * pout_ref[here]
                out0 = now * in0 + jnp.where(live, start, 0.0)
            else:
                in0 = jnp.where(live, up_ref[parity * lev + j, :rows], 0.0)
                in1 = jnp.where(live, up_ref[parity * lev + j, rows:], 0.0)
                out0 = now * in0
            out1 = now * in1 + back * in0 + carry * out0
            up_ref[parity * lev + j] = jnp.zeros((2 * rows, LANES), jnp.float32)
            flow_ref[pl.ds(here * 2 * rows, rows), :] = out0
            flow_ref[pl.ds(here * 2 * rows + rows, rows), :] = out1
            target = (1 - parity) * lev + down_ref[b]
            up_ref[target, :rows] += out0
            up_ref[target, rows:] += out1
            return 0

        lax.fori_loop(0, lev, block, 0, unroll=4)

    def observe(seg):
        def one(g, _):
            slot = gauge_ref[seg * gauges + g]
            row = (slot // LANES) * (2 * rows) + slot % rows
            row_ref[pl.ds(g, 1), :] = flow_ref[pl.ds(row, 1), :]
            row_ref[pl.ds(gauges + g, 1), :] = flow_ref[pl.ds(row + rows, 1), :]
            return 0

        lax.fori_loop(0, gauges, one, 0, unroll=8)
        pick = pick_ref[seg]
        for h in range(2):
            kept = row_ref[h * gauges : (h + 1) * gauges, :] * pick
            out_ref[seg, h * members : (h + 1) * members, :] = lax.dot_general(
                fold_ref[...], kept, (((1,), (1,)), ((), ())),
                precision=exact_mode, preferred_element_type=jnp.float32,
            )

    lax.fori_loop(0, 2 * lev, clear, 0, unroll=8)

    def nothing(seg, _):
        out_ref[seg] = jnp.zeros(out_ref.shape[1:], jnp.float32)
        return 0

    lax.fori_loop(0, first, nothing, 0)
    for level in range(level_count):
        sweep(first, level, level % 2, True)
    observe(first)

    def later(seg, _):
        for level in range(level_count):
            sweep(seg, level, level % 2, False)
        observe(seg)
        return 0

    lax.fori_loop(first + 1, seg_count, later, 0)


def invert_small(d):
    size = d.shape[0]
    lane = lax.broadcasted_iota(jnp.int32, d.shape, 1)
    sub = lax.broadcasted_iota(jnp.int32, d.shape, 0)
    for j in range(size):
        inv = 1.0 / d[j : j + 1, j : j + 1]
        row = jnp.where(lane[:1] == j, 1.0, d[j : j + 1, :]) * inv
        col = d[:, j : j + 1]
        rest = jnp.where(lane == j, 0.0, d) - col * row
        d = jnp.where(sub == j, row, rest)
    return d


def exact_dot(a, b):
    return jnp.dot(a, b, precision=exact_mode, preferred_element_type=jnp.float32)


def solve_body(n, size, chunk_ref, cross_ref, out_ref, a_ref, l_ref):
    total = n * size
    sub = lax.broadcasted_iota(jnp.int32, (size, total), 0)
    lane = lax.broadcasted_iota(jnp.int32, (size, total), 1)
    for q in range(n):
        rows = chunk_ref[q]
        pieces = [rows[:, (p ^ q) * size : ((p ^ q) + 1) * size] for p in range(n)]
        rows = jnp.concatenate(pieces, axis=1)
        a_ref[q * size : (q + 1) * size, :] = rows + jnp.where(lane == sub + q * size, 1.0, 0.0)
    out_ref[...] = cross_ref[...]
    for k in range(n):
        span = slice(k * size, (k + 1) * size)
        left = (k * size // LANES) * LANES
        inverse = invert_small(a_ref[span, span])
        right = exact_dot(inverse, out_ref[span, :])
        l_ref[...] = a_ref[:, span]
        l_ref[span, :] = jnp.zeros((size, size), jnp.float32)
        column = l_ref[...]
        if k < n - 1:
            top = exact_dot(inverse, a_ref[span, left:])
            a_ref[:, left:] -= exact_dot(column, top)
            a_ref[span, left:] = top
        out_ref[...] -= exact_dot(column, right)
        out_ref[span, :] = right


def inverse_sinh(values):
    return jnp.log(values + jnp.sqrt(values * values + 1.0))


def shards(
    prior_params, lateral_flow, inflow_start, outflow_start, reach_count, downstream,
    gauge_reach, observed, obs_var, obs_noise,
):
    md, param_count, block_dev = prior_params.shape
    hours = lateral_flow.shape[1]
    gauges = gauge_reach.shape[0]
    basins = lax.axis_size("basin")
    n_member = lax.axis_size("member")
    members = md * n_member
    level_count = block_dev // BLK_LEV
    packs = LANES // md
    f32 = jnp.float32

    prior_all = permuted_gather(prior_params, "member").reshape(members, param_count * block_dev)

    meta = jnp.concatenate(
        [
            prior_params[:, :2, :].reshape(md * 2, block_dev),
            downstream.astype(f32)[None],
            reach_count.astype(f32)[None],
            gauge_reach.astype(f32).reshape(-1, block_dev),
        ],
        0,
    )
    extra = -meta.shape[0] % 8
    meta = jnp.concatenate([meta, jnp.zeros((extra, block_dev), f32)], 0)
    meta_all = exchange(meta, "basin", 1)
    pair = meta_all[:, : md * 2].reshape(basins, md, 2, block_dev)
    down_all = meta_all[:, md * 2].reshape(-1).astype(jnp.int32)
    count_all = meta_all[:, md * 2 + 1].reshape(-1).astype(jnp.int32)
    gauge_rows = gauges // block_dev
    gauge_all = (
        meta_all[:, md * 2 + 2 : md * 2 + 2 + gauge_rows].reshape(basins, gauges).astype(jnp.int32)
    )

    storage = 0.02 + 0.1 * jax.nn.sigmoid(pair[:, :, 0])
    weighting = 0.2 * jax.nn.sigmoid(pair[:, :, 1])
    denominator = storage * (1.0 - weighting) + 0.5

    def spread_lanes(values):
        turned = jnp.swapaxes(values, -1, -2)
        return jnp.tile(turned, (1, 1, packs)).reshape(-1, LANES)

    weight_now = spread_lanes((0.5 - storage * weighting) / denominator)
    weight_back = spread_lanes((0.5 + storage * weighting) / denominator)
    weight_carry = spread_lanes((storage * (1.0 - weighting) - 0.5) / denominator)

    modes = param_count - 2
    turned = jnp.transpose(0.2 * prior_params[:, 2:, :], (1, 2, 0))
    turned = jnp.tile(turned, (1, 1, packs))
    lane_pos = jnp.arange(LANES, dtype=f32)
    orders = jnp.arange(modes, dtype=f32)
    cosine = jnp.cos(math.pi * orders[:, None] * (lane_pos[None, :] + 0.5) / LANES)
    cosine = jnp.swapaxes(cosine.reshape(modes, packs, md), 1, 2)
    cosine = jnp.repeat(cosine, md, axis=2)

    lateral = lateral_flow.reshape(md, hours, block_dev, packs, md)
    lateral = jnp.transpose(lateral, (2, 1, 4, 3, 0)).reshape(block_dev, hours, md, LANES)

    def start_state(values):
        shaped = jnp.swapaxes(values.reshape(block_dev, packs, md), 1, 2)
        return jnp.repeat(shaped, md, axis=2)

    phase = jnp.arange(LANES, dtype=jnp.int32) // md
    pick = ((gauge_all % LANES) // md)[:, :, None] == phase[None, None, :]
    fold = (
        jnp.arange(LANES, dtype=jnp.int32)[None, :] % md == jnp.arange(md, dtype=jnp.int32)[:, None]
    )
    basin_idx = lax.axis_index("basin").astype(jnp.int32).reshape(1)

    parts = pl.pallas_call(
        functools.partial(route_body, basins, level_count, md, gauges),
        out_shape=jax.ShapeDtypeStruct((basins, 2 * md, gauges), f32),
        in_specs=[smem_spec()] * 4 + [vmem_spec()] * 10,
        out_specs=vmem_spec(),
        scratch_shapes=[
            VMEM((2 * BLK_LEV, 2 * md, LANES), f32),
            VMEM((block_dev * 2 * md, LANES), f32),
            VMEM((2 * gauges, LANES), f32),
        ],
        cost_estimate=pl.CostEstimate(
            flops=40_000_000, bytes_accessed=60_000_000, transcendentals=0
        ),
        name="route",
    )(
        basin_idx, down_all, count_all, gauge_all.reshape(-1),
        weight_now, weight_back, weight_carry, turned, cosine, lateral,
        start_state(inflow_start), start_state(outflow_start), pick.astype(f32), fold.astype(f32),
    )
    arrived = exchange(parts, "basin", 2, spread_out=True)
    flows = jnp.sum(arrived, 0)
    pred = inverse_sinh(flows).reshape(hours, md, gauges)
    predicted = jnp.swapaxes(pred, 0, 1)
    flat = jnp.concatenate([pred[h] for h in range(hours)], axis=1)
    pred_all = doubling_gather(flat, "member", 3).reshape(members, hours * gauges)

    spread = jnp.sqrt(obs_var).reshape(1, -1)
    spread_root = math.sqrt(members - 1.0)
    noise = jnp.concatenate([obs_noise[:, h] for h in range(hours)], axis=1)
    innovation = (observed.reshape(1, -1) + 2.0 * spread * noise - flat) / (2.0 * spread)
    mean_pred = jnp.sum(pred_all, 0, keepdims=True) / members
    scaled_all = (pred_all - mean_pred) / (spread_root * (2.0 * spread))
    scaled = (flat - mean_pred) / (spread_root * (2.0 * spread))
    both = jnp.concatenate([scaled, innovation], 0)
    part = lax.dot_general(
        both, scaled_all, (((1,), (1,)), ((), ())),
        precision=exact_mode, preferred_element_type=f32,
    )
    summed = jnp.sum(exchange(part, "basin", 4), 0)
    chunks = doubling_gather(summed[:md], "member", 5)
    gain = pl.pallas_call(
        functools.partial(solve_body, n_member, md),
        out_shape=jax.ShapeDtypeStruct((members, md), f32),
        in_specs=[vmem_spec()] * 2,
        out_specs=vmem_spec(),
        scratch_shapes=[VMEM((members, members), f32), VMEM((members, md), f32)],
        cost_estimate=pl.CostEstimate(
            flops=40_000_000, bytes_accessed=60_000_000, transcendentals=0
        ),
        name="solve",
    )(chunks, summed[md:].T)

    mean_prior = jnp.sum(prior_all, 0, keepdims=True) / members
    anomaly = (prior_all - mean_prior) / spread_root
    change = lax.dot_general(
        gain, anomaly, (((0,), (0,)), ((), ())), precision=exact_mode, preferred_element_type=f32
    )
    posterior = prior_params + change.reshape(md, param_count, block_dev)
    return (posterior, predicted)


def solution(mesh):
    return jax.shard_map(
        shards,
        mesh=mesh,
        in_specs=(
            P("member", None, "basin"),
            P("member", None, "basin"),
            P("basin"),
            P("basin"),
            P("basin"),
            P("basin"),
            P("basin"),
            P(None, "basin"),
            P(None, "basin"),
            P("member", None, "basin"),
        ),
        out_specs=(P("member", None, "basin"), P("member", None, "basin")),
        check_vma=False,
    )
```

time: 471 us -> 195 us (0.41)
  waiting for transfers between devices: 172 us -> 7.19 us
  Pallas kernels: 0 us -> 113 us
  other arithmetic: 102 us -> 13.8 us
  starting transfers between devices: 80.2 us -> 4.27 us
  matrix products: 27.6 us -> 2.83 us
  between operations: 15.4 us -> 1.1 us
  blocking collectives: 13.6 us -> 0 us
    pallas_call x0 -> x7, Pallas kernels: none -> 113 us  [the longest x1 30.9 us: shards(): pl.pallas_call(functools.partial(route_body, basins, level_count, md, gau...]
    ppermute x14 -> x3, starting transfers between devices: 79.8 us -> 4.27 us  [permuted_gather(): other = lax.ppermute(held, axis, [(i, i ^ bit) for i in range(n)])]
    all_gather x3 -> x0, waiting for transfers between devices: 64.2 us -> none  [the longest x1 23.8 us: shards(): lax.all_gather(scaled, 'member', axis=0, tiled=True)]
    another operation x11 -> x0, other arithmetic: 54.6 us -> none  [the longest x6 34.1 us: solve_gram(): factor = jnp.linalg.cholesky(gram_matrix)]
    ppermute x14 -> x3, waiting for transfers between devices: 61.7 us -> 7.19 us  [permuted_gather(): other = lax.ppermute(held, axis, [(i, i ^ bit) for i in range(n)])]
    psum x1 -> x0, waiting for transfers between devices: 45.1 us -> none  [shards(): gram_matrix, cross_matrix = lax.psum((gram_part, cross_part), 'basin')]
    dot_general x20 -> x2, matrix products: 25.4 us -> 2.83 us  [the longest x1 1.72 us: shards(): lax.dot_general(both, scaled_all, (((1,), (1,)), ((), ())), precision=exa...]
    reshape x1 -> x7, local copies, waits for them, and re-layouts: 6.63 us -> 23.2 us  [the longest x1 12.4 us: shards(): lateral = lateral_flow.reshape(md, hours, block_dev, packs, md)]
  transfers between devices with their start and end apart: 18 -> 3, of which waited for: 18 -> 1; matrix products, arithmetic and copies ran while one was open for 2% -> 34% of each run, Pallas kernels for 0% -> 58%
where the time goes in v1:
time: 195 us; the launch traced here: 194 us
  Pallas kernels  113 us (58%)
  local copies, waits for them, and re-layouts  52.6 us (27%)
  other arithmetic  13.8 us (7%)
  waiting for transfers between devices  7.19 us (4%)
  starting transfers between devices  4.27 us (2%)
  matrix products  2.83 us (1%)
    pallas_call x1, Pallas kernels, shards(): pl.pallas_call(functools.partial(route_body, basins, level_count, md, gau...  30.9 us
    pallas_call x2, Pallas kernels, doubling_gather(): pl.pallas_call(functools.partial(doubling_body, axis, n), out_shape=jax.S...  30.1 us
    pallas_call x1, Pallas kernels, shards(): pl.pallas_call(functools.partial(solve_body, n_member, md), out_shape=jax...  27.6 us
    pallas_call x3, Pallas kernels, exchange(): pl.pallas_call(functools.partial(exchange_body, axis, n, spread_out), out...  23.9 us
    reshape x1, local copies, waits for them, and re-layouts, shards(): lateral = lateral_flow.reshape(md, hours, block_dev, packs, md)  12.4 us
    transpose x1, local copies, waits for them, and re-layouts, shards(): jnp.transpose(lateral, (2, 1, 4, 3, 0)).reshape(block_dev, hours, md, LANES)  11.7 us
    unnamed x24, local copies, waits for them, and re-layouts  8.9 us
    ppermute x3, waiting for transfers between devices, permuted_gather(): other = lax.ppermute(held, axis, [(i, i ^ bit) for i in range(n)])  7.19 us
  transfers between devices with their start and end apart: 3, of which 1 were waited for; matrix products, arithmetic and copies ran while one was open for 34% of the time, Pallas kernels for 58%

profile of v1, /device:TPU:0, one launch (start us, length us, event | category | flops | bytes accessed | tf_op | source)
XLA Modules:
  0.0 194.2 jit_solution(7781006337024646609)
XLA Ops:
  0.6 4.1 %collective-permute-start = (f32[1,32,8,128]{3,2,1,0:T(8,128)}, f32[1,32,8,128]{3,2,1,0:T(8,128)S(1)}, u32[]{:S(2)}, u32[]{:S(2)}) collective-permute-start(f32[1,32,8,128]{3,2,1,0:T(8,128)} %bitcast.140), channel_id=1, source_target_pairs={{0,16},{4,20},{8,24},{12,28},{16,0},{20,4},{24,8},{28,12},{1,17},{... | collective-permute-start | bytes 393224 | tf_op jit(solution)/shard_map/ppermute | solution.py:130
  4.8 0.9 slice.44
  7.1 1.2 concatenate.23.x_ref
  8.3 6.8 %exchange_1.1 = f32[4,72,128]{2,1,0:T(8,128)} custom-call(f32[72,128]{1,0:T(8,128)} %concatenate.23.x_ref), custom_call_target="tpu_custom_call" | custom-call | tf_op jit(solution)/shard_map/exchange_1/pallas_call | solution.py:60
  15.1 0.9 slice.48
  16.0 1.3 fusion.18
  17.4 1.4 slice_convert_fusion.1
  18.8 0.9 multiply_bitcast_fusion
  20.0 0.8 copy.100.carry_ref
  21.9 0.8 copy.99.back_ref
  22.8 6.6 %copy.94 = f32[32,2,16384]{2,0,1:T(8,128)} copy(f32[32,2,16384]{2,1,0:T(2,128)} %param.11) | data formatting | bytes 8388608 | tf_op args[1]
  29.4 12.4 %reshape.219 = f32[32,2,128,4,32]{4,3,2,0,1:T(4,128)} reshape(f32[32,2,16384]{2,0,1:T(8,128)} %copy.94) | data formatting | bytes 8388608 | tf_op jit(solution)/shard_map/reshape | solution.py:335
  41.8 11.7 %copy.95 = f32[128,2,32,4,32]{0,4,3,2,1:T(8,128)} copy(f32[128,2,32,4,32]{2,3,0,4,1:T(4,128)} %bitcast.136) | data formatting | bytes 8388608 | tf_op jit(solution)/shard_map/transpose | solution.py:336
  53.5 5.5 %copy.102.lat_ref = f32[128,2,32,128]{3,2,1,0:T(8,128)} copy(f32[128,2,32,128]{0,3,2,1:T(8,128)} %bitcast.137) | data formatting | bytes 8388608 | tf_op jit(solution)/shard_map/reshape | solution.py:336
  59.5 2.1 %copy.103.pin_ref = f32[128,32,128]{2,1,0:T(8,128)} copy(f32[128,32,128]{0,2,1:T(8,128)S(1)} %bitcast.138) | data formatting | bytes 4194304 | tf_op jit(solution)/shard_map/reshape | solution.py:340
  62.0 2.0 %copy.104.pout_ref = f32[128,32,128]{2,1,0:T(8,128)} copy(f32[128,32,128]{0,2,1:T(8,128)S(1)} %bitcast.139) | data formatting | bytes 4194304 | tf_op jit(solution)/shard_map/reshape | solution.py:340
  64.1 0.9 copy.101.par_ref
  65.7 0.8 reshape.218.cos_ref
  67.1 1.4 compare_convert_fusion.pick_ref
  68.5 30.9 %route.1.x_ref = f32[4,64,512]{2,1,0:T(8,128)} custom-call(s32[1]{0:T(128)} %bitcast.basin_ref, s32[512]{0:T(512)} %bitcast.167, s32[512]{0:T(512)} %bitcast.166, s32[2048]{0:T(1024)} %bitcast.163, f32[512,128]{1,0:T(8,128)} %copy.98.now_ref, f32[512,128]{1,0:T(8,128)} %copy.99.back_ref, f32[512,128]{1,0:T(8,128)} %copy.100.carry_ref, ...), custom_call_target="tpu_custom_call" | custom-call | flops 40000000 | bytes 60000000 | tf_op jit(solution)/shard_map/route/pallas_call | solution.py:349
  99.5 8.7 %exchange_2.1 = f32[4,64,512]{2,1,0:T(8,128)} custom-call(f32[4,64,512]{2,1,0:T(8,128)} %route.1.x_ref), custom_call_target="tpu_custom_call" | custom-call | tf_op jit(solution)/shard_map/exchange_2/pallas_call | solution.py:60
  108.2 1.1 reduce_sum.74
  110.0 18.0 %doubling_3.1 = f32[8,32,1024]{2,1,0:T(8,128)} custom-call(f32[32,1024]{1,0:T(8,128)} %pad_maximum_fusion.3.x_ref), custom_call_target="tpu_custom_call" | custom-call | tf_op jit(solution)/shard_map/doubling_3/pallas_call | solution.py:111
  128.1 1.3 reduce_sum.75
  129.8 1.4 fusion.2
  131.1 7.2 %collective-permute-done.1 = f32[2,32,8,128]{3,2,1,0:T(8,128)S(1)} collective-permute-done((f32[2,32,8,128]{3,2,1,0:T(8,128)S(1)}, f32[2,32,8,128]{3,2,1,0:T(8,128)S(1)}, u32[]{:S(2)}, u32[]{:S(2)}) %collective-permute-start.1) | collective-permute-done | bytes 262176 | tf_op jit(solution)/shard_map/ppermute | solution.py:130
  138.4 1.7 fusion.3.x_ref
  140.2 8.4 %exchange_4.1 = f32[4,64,256]{2,1,0:T(8,128)} custom-call(f32[64,256]{1,0:T(8,128)} %fusion.3.x_ref), custom_call_target="tpu_custom_call" | custom-call | tf_op jit(solution)/shard_map/exchange_4/pallas_call | solution.py:60
  148.6 1.0 reduce_sum.76
  150.2 12.0 %doubling_5.1.chunk_ref = f32[8,32,256]{2,1,0:T(8,128)} custom-call(f32[32,256]{1,0:T(8,128)} %get-tuple-element.26.x_ref), custom_call_target="tpu_custom_call" | custom-call | tf_op jit(solution)/shard_map/doubling_5/pallas_call | solution.py:111
  163.8 27.6 %solve.1 = f32[256,32]{1,0:T(8,128)} custom-call(f32[8,32,256]{2,1,0:T(8,128)} %doubling_5.1.chunk_ref, f32[256,32]{1,0:T(8,128)} %bitcast.157), custom_call_target="tpu_custom_call" | custom-call | flops 40000000 | bytes 60000000 | tf_op jit(solution)/shard_map/solve/pallas_call | solution.py:389
  192.4 1.1 convolution_add_fusion
  (75 shorter events, 9.9 us)
Async XLA Ops:
  0.6 129.0 %collective-permute-start = (f32[1,32,8,128]{3,2,1,0:T(8,128)}, f32[1,32,8,128]{3,2,1,0:T(8,128)S(1)}, u32[]{:S(2)}, u32[]{:S(2)}) collective-permute-start(f32[1,32,8,128]{3,2,1,0:T(8,128)} %bitcast.140), channel_id=1, source_target_pairs={{0,16},{4,20},{8,24},{12,28},{16,0},{20,4},{24,8},{28,12},{1,17},{... | collective-permute-start | bytes 393224 | tf_op jit(solution)/shard_map/ppermute | solution.py:130
  53.5 5.5 %copy-start.3 = (f32[16384]{0:T(1024)S(1)}, f32[16384]{0:T(1024)}, u32[]{:S(2)}) copy-start(f32[16384]{0:T(1024)} %param.12) | copy-start | bytes 196612
  59.0 2.5 %copy-start.4 = (f32[16384]{0:T(1024)S(1)}, f32[16384]{0:T(1024)}, u32[]{:S(2)}) copy-start(f32[16384]{0:T(1024)} %param.13) | copy-start | bytes 196612
  99.4 29.9 %copy-start.2 = (f32[32,2,512]{2,1,0:T(2,128)S(1)}, f32[32,2,512]{2,1,0:T(2,128)}, u32[]{:S(2)}) copy-start(f32[32,2,512]{2,1,0:T(2,128)} %param.19) | copy-start | bytes 393220
  99.4 30.1 %copy-start.5 = (f32[2,512]{1,0:T(2,128)S(1)}, f32[2,512]{1,0:T(2,128)}, u32[]{:S(2)}) copy-start(f32[2,512]{1,0:T(2,128)} %param.18) | copy-start | bytes 12292
  99.4 30.1 %copy-start.6 = (f32[2,512]{1,0:T(2,128)S(1)}, f32[2,512]{1,0:T(2,128)}, u32[]{:S(2)}) copy-start(f32[2,512]{1,0:T(2,128)} %param.17) | copy-start | bytes 12292
  99.5 30.2 %copy-start = (f32[32,8,128]{2,1,0:T(8,128)S(1)}, f32[32,8,128]{2,1,0:T(8,128)}, u32[]{:S(2)}) copy-start(f32[32,8,128]{2,1,0:T(8,128)} %param.10) | copy-start | bytes 393220
  129.7 8.6 %collective-permute-start.1 = (f32[2,32,8,128]{3,2,1,0:T(8,128)S(1)}, f32[2,32,8,128]{3,2,1,0:T(8,128)S(1)}, u32[]{:S(2)}, u32[]{:S(2)}) collective-permute-start(f32[2,32,8,128]{3,2,1,0:T(8,128)S(1)} %pad_maximum_fusion.2), channel_id=1, source_target_pairs={{0,8},{4,12},{8,0},{12,4},{16,24},{20,28},{24,16},{28,20},{1,9},{5... | collective-permute-start | bytes 786440 | tf_op jit(solution)/shard_map/ppermute | solution.py:130
  138.4 53.2 %collective-permute-start.2 = (f32[4,32,8,128]{3,2,1,0:T(8,128)S(1)}, f32[4,32,8,128]{3,2,1,0:T(8,128)S(1)}, u32[]{:S(2)}, u32[]{:S(2)}) collective-permute-start(f32[4,32,8,128]{3,2,1,0:T(8,128)S(1)} %pad_maximum_fusion.1), channel_id=1, source_target_pairs={{0,4},{4,0},{8,12},{12,8},{16,20},{20,16},{24,28},{28,24},{1,5},{5... | collective-permute-start | bytes 1572872 | tf_op jit(solution)/shard_map/ppermute | solution.py:130
  191.4 0.9 copy-start.1

commit v2 on v1

--- a/solution.py
+++ b/solution.py
@@ -4,6 +4,7 @@
 import jax
 import jax.numpy as jnp
 from jax import lax
+import numpy as np
 from jax.experimental import pallas as pl
 from jax.experimental.pallas import tpu as pltpu
 from jax.sharding import PartitionSpec as P
@@ -123,6 +124,61 @@
     )(x)
 
 
+def sum_body(axis, n, x_ref, o_ref, land_ref, sem1, sem2, sem3, sem4):
+    me = lax.axis_index(axis)
+    barrier = pltpu.get_barrier_semaphore()
+    for i in range(1, n):
+        pl.semaphore_signal(
+            barrier, inc=1, device_id={axis: lax.rem(me + i, n)}, device_id_type=MESH
+        )
+    pl.semaphore_wait(barrier, n - 1)
+    copies = []
+    for i in range(1, n):
+        peer = lax.rem(me + i, n)
+        copies.append(
+            pltpu.make_async_remote_copy(
+                src_ref=x_ref.at[peer], dst_ref=land_ref.at[i - 1],
+                send_sem=sem1.at[i - 1], recv_sem=sem2.at[i - 1],
+                device_id={axis: peer}, device_id_type=MESH,
+            )
+        )
+    for copy in copies:
+        copy.start()
+    for copy in copies:
+        copy.wait()
+    total = x_ref[me]
+    for i in range(1, n):
+        total = total + land_ref[i - 1]
+    o_ref[me] = total
+    copies = []
+    for i in range(1, n):
+        copies.append(
+            pltpu.make_async_remote_copy(
+                src_ref=o_ref.at[me], dst_ref=o_ref.at[me],
+                send_sem=sem3.at[i - 1], recv_sem=sem4.at[i - 1],
+                device_id={axis: lax.rem(me + i, n)}, device_id_type=MESH,
+            )
+        )
+    for copy in copies:
+        copy.start()
+    for copy in copies:
+        copy.wait()
+
+
+def sum_over(x, axis, collective_id):
+    n = lax.axis_size(axis)
+    return pl.pallas_call(
+        functools.partial(sum_body, axis, n),
+        out_shape=jax.ShapeDtypeStruct(x.shape, x.dtype),
+        in_specs=[vmem_spec()],
+        out_specs=vmem_spec(),
+        scratch_shapes=[VMEM((n - 1,) + x.shape[1:], x.dtype)]
+        + [pltpu.SemaphoreType.DMA((n - 1,))] * 4,
+        compiler_params=pltpu.CompilerParams(collective_id=collective_id, has_side_effects=True),
+        name=f"sum_{collective_id}",
+    )(x)
+
+
 def permuted_gather(x, axis):
     n = lax.axis_size(axis)
     held = x[None]
@@ -133,32 +189,86 @@
 
 
 def route_body(
-    seg_count, level_count, members, gauges,
-    basin_ref, down_ref, count_ref, gauge_ref,
-    now_ref, back_ref, carry_ref, par_ref, cos_ref, lat_ref, pin_ref, pout_ref, pick_ref, fold_ref,
+    seg_count, level_count, members, gauges, hours, param_count,
+    basin_ref, ints_ref,
+    meta_ref, prior_ref, cos_ref, pin_ref, pout_ref, lat_hbm,
     out_ref,
-    up_ref, flow_ref, row_ref,
+    up_ref, flow_ref, row_ref, now_ref, back_ref, carry_ref, par_ref, raw_ref, ready_ref, sem,
 ):
     first = basin_ref[0]
     lev = BLK_LEV
     seg_blocks = level_count * lev
     rows = members
+    packs = LANES // members
     shape = (rows, LANES)
-    place = (lax.broadcasted_iota(jnp.int32, shape, 1) // members) * members
-    place = place + lax.broadcasted_iota(jnp.int32, shape, 0)
-    zero = jnp.zeros(shape, jnp.float32)
+    lane = lax.broadcasted_iota(jnp.int32, shape, 1)
+    place = (lane // members) * members + lax.broadcasted_iota(jnp.int32, shape, 0)
+
+    def fetch(m):
+        return pltpu.make_async_copy(lat_hbm.at[m], raw_ref.at[:, m], sem.at[m])
+
+    for m in range(members):
+        fetch(m).start()
 
     def clear(i, _):
         up_ref[i] = jnp.zeros((2 * rows, LANES), jnp.float32)
         return 0
 
+    lax.fori_loop(0, 2 * lev, clear, 0, unroll=8)
+
+    def turned(values):
+        return jnp.concatenate([values] * packs, axis=0).T
+
+    def coefficients(seg, _):
+        storage = 0.02 + 0.1 * jax.nn.sigmoid(meta_ref[seg, :members, :])
+        weighting = 0.2 * jax.nn.sigmoid(meta_ref[seg, members : 2 * members, :])
+        den = storage * (1.0 - weighting) + 0.5
+        span = pl.ds(pl.multiple_of(seg * seg_blocks, seg_blocks), seg_blocks)
+        now_ref[span, :] = turned((0.5 - storage * weighting) / den)
+        back_ref[span, :] = turned((0.5 + storage * weighting) / den)
+        carry_ref[span, :] = turned((storage * (1.0 - weighting) - 0.5) / den)
+        return 0
+
+    lax.fori_loop(first, seg_count, coefficients, 0)
+    for k in range(param_count - 2):
+        par_ref[k] = turned(0.2 * prior_ref[:, 2 + k, :])
+    for m in range(members):
+        fetch(m).wait()
+
+    def place_group(tiles):
+        flat = jnp.concatenate(tiles, axis=0).T
+        strips = [flat[q * rows : (q + 1) * rows] for q in range(packs)]
+        made = []
+        for i in range(packs):
+            total = None
+            for q in range(packs):
+                shift = ((q - i) * members) % LANES
+                piece = pltpu.roll(strips[q], shift, 1) if shift else strips[q]
+                total = piece if total is None else jnp.where(lane // members == q, piece, total)
+            made.append(total)
+        return made
+
+    def relayout(group, _):
+        base = group * packs
+        for h in range(hours):
+            tiles = [raw_ref[(base + i) * hours + h] for i in range(packs)]
+            for i, tile in enumerate(place_group(tiles)):
+                ready_ref[base + i, h] = tile
+        for n, ref in enumerate((pin_ref, pout_ref)):
+            tiles = [
+                jnp.broadcast_to(ref[pl.ds(base + i, 1), :], shape) for i in range(packs)
+            ]
+            for i, tile in enumerate(place_group(tiles)):
+                ready_ref[base + i, hours + n] = tile
+        return 0
+
+    lax.fori_loop(0, seg_blocks // packs, relayout, 0, unroll=2)
+
     def sweep(seg, level, parity, own):
-        base = seg * seg_blocks + level * lev
-
         def block(j, _):
-            b = base + j
             here = level * lev + j
-            live = place < count_ref[b]
+            b = seg * seg_blocks + here
+            live = place < ints_ref[seg, 1, here]
             now = now_ref[pl.ds(b, 1), :]
             back = back_ref[pl.ds(b, 1), :]
             carry = carry_ref[pl.ds(b, 1), :]
@@ -167,14 +277,14 @@
                 for k in range(1, cos_ref.shape[0]):
                     expo = expo + cos_ref[k] * par_ref[k, pl.ds(here, 1), :]
                 scale = jnp.exp(expo)
-                add0 = lat_ref[here, 0] * scale
-                add1 = lat_ref[here, 1] * scale
+                add0 = ready_ref[here, 0] * scale
+                add1 = ready_ref[here, 1] * scale
                 if level > 0:
                     add0 = add0 + up_ref[parity * lev + j, :rows]
                     add1 = add1 + up_ref[parity * lev + j, rows:]
                 in0 = jnp.where(live, add0, 0.0)
                 in1 = jnp.where(live, add1, 0.0)
-                start = back * pin_ref[here] + carry * pout_ref[here]
+                start = back * ready_ref[here, 2] + carry * ready_ref[here, 3]
                 out0 = now * in0 + jnp.where(live, start, 0.0)
             else:
                 in0 = jnp.where(live, up_ref[parity * lev + j, :rows], 0.0)
@@ -184,31 +294,34 @@
             up_ref[parity * lev + j] = jnp.zeros((2 * rows, LANES), jnp.float32)
             flow_ref[pl.ds(here * 2 * rows, rows), :] = out0
             flow_ref[pl.ds(here * 2 * rows + rows, rows), :] = out1
-            target = (1 - parity) * lev + down_ref[b]
+            target = (1 - parity) * lev + ints_ref[seg, 0, here]
             up_ref[target, :rows] += out0
             up_ref[target, rows:] += out1
             return 0
 
         lax.fori_loop(0, lev, block, 0, unroll=4)
 
+    fold = lax.broadcasted_iota(jnp.int32, shape, 0) == lane % members
+    fold = fold.astype(jnp.float32)
+    one_lane = lax.broadcasted_iota(jnp.int32, (1, LANES), 1) // members
+
     def observe(seg):
         def one(g, _):
-            slot = gauge_ref[seg * gauges + g]
+            slot = ints_ref[seg, 2 + g // LANES, g % LANES]
             row = (slot // LANES) * (2 * rows) + slot % rows
-            row_ref[pl.ds(g, 1), :] = flow_ref[pl.ds(row, 1), :]
-            row_ref[pl.ds(gauges + g, 1), :] = flow_ref[pl.ds(row + rows, 1), :]
+            keep = one_lane == (slot % LANES) // rows
+            row_ref[pl.ds(g, 1), :] = jnp.where(keep, flow_ref[pl.ds(row, 1), :], 0.0)
+            row_ref[pl.ds(gauges + g, 1), :] = jnp.where(
+                keep, flow_ref[pl.ds(row + rows, 1), :], 0.0
+            )
             return 0
 
         lax.fori_loop(0, gauges, one, 0, unroll=8)
-        pick = pick_ref[seg]
         for h in range(2):
-            kept = row_ref[h * gauges : (h + 1) * gauges, :] * pick
             out_ref[seg, h * members : (h + 1) * members, :] = lax.dot_general(
-                fold_ref[...], kept, (((1,), (1,)), ((), ())),
+                fold, row_ref[h * gauges : (h + 1) * gauges, :], (((1,), (1,)), ((), ())),
                 precision=exact_mode, preferred_element_type=jnp.float32,
             )
-
-    lax.fori_loop(0, 2 * lev, clear, 0, unroll=8)
 
     def nothing(seg, _):
         out_ref[seg] = jnp.zeros(out_ref.shape[1:], jnp.float32)
@@ -232,12 +345,21 @@
     size = d.shape[0]
     lane = lax.broadcasted_iota(jnp.int32, d.shape, 1)
     sub = lax.broadcasted_iota(jnp.int32, d.shape, 0)
-    for j in range(size):
-        inv = 1.0 / d[j : j + 1, j : j + 1]
-        row = jnp.where(lane[:1] == j, 1.0, d[j : j + 1, :]) * inv
-        col = d[:, j : j + 1]
-        rest = jnp.where(lane == j, 0.0, d) - col * row
-        d = jnp.where(sub == j, row, rest)
+    for j in range(0, size, 2):
+        i = j + 1
+        row0, row1 = d[j : j + 1, :], d[i : i + 1, :]
+        col0, col1 = d[:, j : j + 1], d[:, i : i + 1]
+        a, b = d[j : j + 1, j : j + 1], d[j : j + 1, i : i + 1]
+        e, f = d[i : i + 1, j : j + 1], d[i : i + 1, i : i + 1]
+        inv = 1.0 / (a * f - b * e)
+        at0, at1 = lane[:1] == j, lane[:1] == i
+        row0 = jnp.where(at0, 1.0, jnp.where(at1, 0.0, row0))
+        row1 = jnp.where(at0, 0.0, jnp.where(at1, 1.0, row1))
+        new0 = (f * row0 - b * row1) * inv
+        new1 = (a * row1 - e * row0) * inv
+        kept = jnp.where((lane == j) | (lane == i), 0.0, d)
+        rest = kept - (col0 * new0 + col1 * new1)
+        d = jnp.where(sub == j, new0, jnp.where(sub == i, new1, rest))
     return d
 
 
@@ -245,16 +367,12 @@
     return jnp.dot(a, b, precision=exact_mode, preferred_element_type=jnp.float32)
 
 
-def solve_body(n, size, chunk_ref, cross_ref, out_ref, a_ref, l_ref):
+def solve_body(n, size, sums_ref, out_ref, a_ref, l_ref):
     total = n * size
-    sub = lax.broadcasted_iota(jnp.int32, (size, total), 0)
-    lane = lax.broadcasted_iota(jnp.int32, (size, total), 1)
-    for q in range(n):
-        rows = chunk_ref[q]
-        pieces = [rows[:, (p ^ q) * size : ((p ^ q) + 1) * size] for p in range(n)]
-        rows = jnp.concatenate(pieces, axis=1)
-        a_ref[q * size : (q + 1) * size, :] = rows + jnp.where(lane == sub + q * size, 1.0, 0.0)
-    out_ref[...] = cross_ref[...]
+    sub = lax.broadcasted_iota(jnp.int32, (total, total), 0)
+    lane = lax.broadcasted_iota(jnp.int32, (total, total), 1)
+    a_ref[...] = sums_ref[:total, :] + jnp.where(lane == sub, 1.0, 0.0)
+    out_ref[...] = sums_ref[total : total + size, :].T
     for k in range(n):
         span = slice(k * size, (k + 1) * size)
         left = (k * size // LANES) * LANES
@@ -291,79 +409,57 @@
 
     prior_all = permuted_gather(prior_params, "member").reshape(members, param_count * block_dev)
 
+    gauge_rows = gauges // block_dev
+    extra = -(md * 2 + 2 + gauge_rows) % 8
     meta = jnp.concatenate(
         [
-            prior_params[:, :2, :].reshape(md * 2, block_dev),
+            prior_params[:, 0, :],
+            prior_params[:, 1, :],
             downstream.astype(f32)[None],
             reach_count.astype(f32)[None],
             gauge_reach.astype(f32).reshape(-1, block_dev),
+            jnp.zeros((extra, block_dev), f32),
         ],
         0,
     )
-    extra = -meta.shape[0] % 8
-    meta = jnp.concatenate([meta, jnp.zeros((extra, block_dev), f32)], 0)
     meta_all = exchange(meta, "basin", 1)
-    pair = meta_all[:, : md * 2].reshape(basins, md, 2, block_dev)
-    down_all = meta_all[:, md * 2].reshape(-1).astype(jnp.int32)
-    count_all = meta_all[:, md * 2 + 1].reshape(-1).astype(jnp.int32)
-    gauge_rows = gauges // block_dev
-    gauge_all = (
-        meta_all[:, md * 2 + 2 : md * 2 + 2 + gauge_rows].reshape(basins, gauges).astype(jnp.int32)
-    )
-
-    storage = 0.02 + 0.1 * jax.nn.sigmoid(pair[:, :, 0])
-    weighting = 0.2 * jax.nn.sigmoid(pair[:, :, 1])
-    denominator = storage * (1.0 - weighting) + 0.5
-
-    def spread_lanes(values):
-        turned = jnp.swapaxes(values, -1, -2)
-        return jnp.tile(turned, (1, 1, packs)).reshape(-1, LANES)
-
-    weight_now = spread_lanes((0.5 - storage * weighting) / denominator)
-    weight_back = spread_lanes((0.5 + storage * weighting) / denominator)
-    weight_carry = spread_lanes((storage * (1.0 - weighting) - 0.5) / denominator)
+    ints_all = meta_all[:, md * 2 : md * 2 + 2 + gauge_rows].astype(jnp.int32)
 
     modes = param_count - 2
-    turned = jnp.transpose(0.2 * prior_params[:, 2:, :], (1, 2, 0))
-    turned = jnp.tile(turned, (1, 1, packs))
-    lane_pos = jnp.arange(LANES, dtype=f32)
-    orders = jnp.arange(modes, dtype=f32)
-    cosine = jnp.cos(math.pi * orders[:, None] * (lane_pos[None, :] + 0.5) / LANES)
-    cosine = jnp.swapaxes(cosine.reshape(modes, packs, md), 1, 2)
-    cosine = jnp.repeat(cosine, md, axis=2)
-
-    lateral = lateral_flow.reshape(md, hours, block_dev, packs, md)
-    lateral = jnp.transpose(lateral, (2, 1, 4, 3, 0)).reshape(block_dev, hours, md, LANES)
-
-    def start_state(values):
-        shaped = jnp.swapaxes(values.reshape(block_dev, packs, md), 1, 2)
-        return jnp.repeat(shaped, md, axis=2)
-
-    phase = jnp.arange(LANES, dtype=jnp.int32) // md
-    pick = ((gauge_all % LANES) // md)[:, :, None] == phase[None, None, :]
-    fold = (
-        jnp.arange(LANES, dtype=jnp.int32)[None, :] % md == jnp.arange(md, dtype=jnp.int32)[:, None]
-    )
+    lane_pos = np.arange(LANES)
+    cosine = np.cos(math.pi * np.arange(modes)[:, None] * (lane_pos[None, :] + 0.5) / LANES)
+    cosine = np.swapaxes(cosine.reshape(modes, packs, md), 1, 2)
+    cosine = jnp.asarray(np.repeat(cosine, md, axis=2), f32)
+
+    lateral = lateral_flow.reshape(md, hours, block_dev, LANES)
+    lateral = jnp.swapaxes(lateral, 1, 2).reshape(md, block_dev * hours, LANES)
     basin_idx = lax.axis_index("basin").astype(jnp.int32).reshape(1)
+    seg_coef = VMEM((basins * block_dev, LANES), f32)
 
     parts = pl.pallas_call(
-        functools.partial(route_body, basins, level_count, md, gauges),
+        functools.partial(route_body, basins, level_count, md, gauges, hours, param_count),
         out_shape=jax.ShapeDtypeStruct((basins, 2 * md, gauges), f32),
-        in_specs=[smem_spec()] * 4 + [vmem_spec()] * 10,
+        in_specs=[smem_spec()] * 2 + [vmem_spec()] * 5 + [pl.BlockSpec(memory_space=pl.ANY)],
         out_specs=vmem_spec(),
         scratch_shapes=[
             VMEM((2 * BLK_LEV, 2 * md, LANES), f32),
             VMEM((block_dev * 2 * md, LANES), f32),
             VMEM((2 * gauges, LANES), f32),
+            seg_coef,
+            seg_coef,
+            seg_coef,
+            VMEM((modes, block_dev, LANES), f32),
+            VMEM((block_dev * hours, md, LANES), f32),
+            VMEM((block_dev, hours + 2, md, LANES), f32),
+            pltpu.SemaphoreType.DMA((md,)),
         ],
         cost_estimate=pl.CostEstimate(
             flops=40_000_000, bytes_accessed=60_000_000, transcendentals=0
         ),
         name="route",
     )(
-        basin_idx, down_all, count_all, gauge_all.reshape(-1),
-        weight_now, weight_back, weight_carry, turned, cosine, lateral,
-        start_state(inflow_start), start_state(outflow_start), pick.astype(f32), fold.astype(f32),
+        basin_idx, ints_all, meta_all, prior_params, cosine,
+        inflow_start.reshape(block_dev, LANES), outflow_start.reshape(block_dev, LANES), lateral,
     )
     arrived = exchange(parts, "basin", 2, spread_out=True)
     flows = jnp.sum(arrived, 0)
@@ -378,25 +474,25 @@
     innovation = (observed.reshape(1, -1) + 2.0 * spread * noise - flat) / (2.0 * spread)
     mean_pred = jnp.sum(pred_all, 0, keepdims=True) / members
     scaled_all = (pred_all - mean_pred) / (spread_root * (2.0 * spread))
-    scaled = (flat - mean_pred) / (spread_root * (2.0 * spread))
-    both = jnp.concatenate([scaled, innovation], 0)
+    row_count = members + md
+    extra = -row_count % (8 * basins)
+    both = jnp.concatenate([scaled_all, innovation, jnp.zeros((extra, flat.shape[1]), f32)], 0)
     part = lax.dot_general(
         both, scaled_all, (((1,), (1,)), ((), ())),
         precision=exact_mode, preferred_element_type=f32,
     )
-    summed = jnp.sum(exchange(part, "basin", 4), 0)
-    chunks = doubling_gather(summed[:md], "member", 5)
+    sums = sum_over(part.reshape(basins, -1, members), "basin", 4).reshape(-1, members)
     gain = pl.pallas_call(
         functools.partial(solve_body, n_member, md),
         out_shape=jax.ShapeDtypeStruct((members, md), f32),
-        in_specs=[vmem_spec()] * 2,
+        in_specs=[vmem_spec()],
         out_specs=vmem_spec(),
         scratch_shapes=[VMEM((members, members), f32), VMEM((members, md), f32)],
         cost_estimate=pl.CostEstimate(
             flops=40_000_000, bytes_accessed=60_000_000, transcendentals=0
         ),
         name="solve",
-    )(chunks, summed[md:].T)
+    )(sums)
 
     mean_prior = jnp.sum(prior_all, 0, keepdims=True) / members
     anomaly = (prior_all - mean_prior) / spread_root

time: 195 us -> 179 us (0.918)
  local copies, waits for them, and re-layouts: 52.6 us -> 6.1 us
  Pallas kernels: 113 us -> 148 us
  other arithmetic: 13.8 us -> 7.92 us
    pallas_call x1, Pallas kernels: 30.9 us -> 65.7 us  [shards(): pl.pallas_call(functools.partial(route_body, basins, level_count, md, gau...]
    reshape x7 -> x0, local copies, waits for them, and re-layouts: 23.2 us -> none  [the longest x1 12.4 us: shards(): lateral = lateral_flow.reshape(md, hours, block_dev, packs, md)]
    pallas_call x0 -> x1, Pallas kernels: none -> 14 us  [sum_over(): pl.pallas_call(functools.partial(sum_body, axis, n), out_shape=jax.ShapeD...]
    transpose x7 -> x0, local copies, waits for them, and re-layouts: 12.1 us -> none  [the longest x1 11.7 us: shards(): jnp.transpose(lateral, (2, 1, 4, 3, 0)).reshape(block_dev, hours, md, LANES)]
    pallas_call x2 -> x1, Pallas kernels: 30.1 us -> 18 us  [doubling_gather(): pl.pallas_call(functools.partial(doubling_body, axis, n), out_shape=jax.S...]
    pallas_call x3 -> x2, Pallas kernels: 23.9 us -> 15.5 us  [exchange(): pl.pallas_call(functools.partial(exchange_body, axis, n, spread_out), out...]
    pallas_call x1, Pallas kernels: 27.6 us -> 34.4 us  [shards(): pl.pallas_call(functools.partial(solve_body, n_member, md), out_shape=jax...]
    unnamed x24 -> x28, local copies, waits for them, and re-layouts: 8.9 us -> 3.82 us
  transfers between devices with their start and end apart: 3 -> 3, of which waited for: 1 -> 1; matrix products, arithmetic and copies ran while one was open for 34% -> 7% of each run, Pallas kernels for 58% -> 83%
where the time goes in v2:
time: 179 us; the launch traced here: 178 us
  Pallas kernels  148 us (83%)
  waiting for transfers between devices  8.41 us (5%)
  other arithmetic  7.92 us (4%)
  local copies, waits for them, and re-layouts  6.1 us (3%)
  starting transfers between devices  4.2 us (2%)
  matrix products  2.95 us (2%)
    pallas_call x1, Pallas kernels, shards(): pl.pallas_call(functools.partial(route_body, basins, level_count, md, gau...  65.7 us
    pallas_call x1, Pallas kernels, shards(): pl.pallas_call(functools.partial(solve_body, n_member, md), out_shape=jax...  34.4 us
    pallas_call x1, Pallas kernels, doubling_gather(): pl.pallas_call(functools.partial(doubling_body, axis, n), out_shape=jax.S...  18 us
    pallas_call x2, Pallas kernels, exchange(): pl.pallas_call(functools.partial(exchange_body, axis, n, spread_out), out...  15.5 us
    pallas_call x1, Pallas kernels, sum_over(): pl.pallas_call(functools.partial(sum_body, axis, n), out_shape=jax.ShapeD...  14 us
    ppermute x3, waiting for transfers between devices, permuted_gather(): other = lax.ppermute(held, axis, [(i, i ^ bit) for i in range(n)])  8.41 us
    ppermute x3, starting transfers between devices, permuted_gather(): other = lax.ppermute(held, axis, [(i, i ^ bit) for i in range(n)])  4.2 us
    unnamed x28, local copies, waits for them, and re-layouts  3.82 us
  transfers between devices with their start and end apart: 3, of which 1 were waited for; matrix products, arithmetic and copies ran while one was open for 7% of the time, Pallas kernels for 83%

profile of v2, /device:TPU:0, one launch (start us, length us, event | category | flops | bytes accessed | tf_op | source)
XLA Modules:
  0.0 178.2 jit_solution(4489083617701764173)
XLA Ops:
  0.6 4.1 %collective-permute-start = (f32[1,32,8,128]{3,2,1,0:T(8,128)}, f32[1,32,8,128]{3,2,1,0:T(8,128)S(1)}, u32[]{:S(2)}, u32[]{:S(2)}) collective-permute-start(f32[1,32,8,128]{3,2,1,0:T(8,128)} %bitcast.62), channel_id=1, source_target_pairs={{0,16},{4,20},{8,24},{12,28},{16,0},{20,4},{24,8},{28,12},{1,17},{... | collective-permute-start | bytes 393224 | tf_op jit(solution)/shard_map/ppermute | solution.py:186
  4.8 1.0 copy.32
  5.7 0.7 convert_bitcast_fusion
  6.4 0.7 convert_bitcast_fusion.1
  7.1 1.8 %concatenate.23.x_ref = f32[72,128]{1,0:T(8,128)} concatenate(f32[32,128]{1,0:T(8,128)S(1)} %get-tuple-element.11, f32[32,128]{1,0:T(8,128)S(1)} %get-tuple-element.10, f32[1,128]{1,0:T(1,128)S(1)} %get-tuple-element.17, f32[1,128]{1,0:T(1,128)S(1)} %get-tuple-element.16, f32[4,128]{1,0:T(4,128)S(1)} %convert_bitcast_fusion, f32[2,128]{1,0:T(2,128)S(1)} %broadcast_in_dim.16), dimensions={0} | concatenate | bytes 73728 | tf_op jit(solution)/shard_map/concatenate | solution.py:414
  8.9 6.8 %exchange_1.1.meta_ref = f32[4,72,128]{2,1,0:T(8,128)} custom-call(f32[72,128]{1,0:T(8,128)} %concatenate.23.x_ref), custom_call_target="tpu_custom_call" | custom-call | tf_op jit(solution)/shard_map/exchange_1/pallas_call | solution.py:61
  15.7 1.3 slice_convert_fusion.ints_ref
  17.1 65.7 %route.1.x_ref = f32[4,64,512]{2,1,0:T(8,128)} custom-call(s32[1]{0:T(128)} %bitcast.basin_ref, s32[4,6,128]{2,1,0:T(8,128)} %slice_convert_fusion.ints_ref, f32[4,72,128]{2,1,0:T(8,128)} %exchange_1.1.meta_ref, f32[32,8,128]{2,1,0:T(8,128)} %prior_ref.1, f32[6,32,128]{2,1,0:T(8,128)} %constant.23.clone.cos_ref, f32[128,128]{1,0:T(8,128)} %bitcast.73, ...), custom_call_target="tpu_custom_call" | custom-call | flops 40000000 | bytes 60000000 | tf_op jit(solution)/shard_map/route/pallas_call | solution.py:439
  82.8 8.7 %exchange_2.1 = f32[4,64,512]{2,1,0:T(8,128)} custom-call(f32[4,64,512]{2,1,0:T(8,128)} %route.1.x_ref), custom_call_target="tpu_custom_call" | custom-call | tf_op jit(solution)/shard_map/exchange_2/pallas_call | solution.py:61
  91.5 1.1 reduce_sum.65
  92.7 0.1 fusion.8
  92.9 0.7 pad_maximum_fusion.4
  93.6 18.0 %doubling_3.1 = f32[8,32,1024]{2,1,0:T(8,128)} custom-call(f32[32,1024]{1,0:T(8,128)} %get-tuple-element.6.x_ref), custom_call_target="tpu_custom_call" | custom-call | tf_op jit(solution)/shard_map/doubling_3/pallas_call | solution.py:112
  111.7 1.4 reduce_sum.66
  113.1 0.1 copy-done
  113.2 0.1 fusion.2
  113.4 0.6 copy-done.1
  114.0 0.1 collective-permute-start.1
  114.1 0.2 subtract_divide_fusion
  114.3 8.4 %collective-permute-done.1 = f32[2,32,8,128]{3,2,1,0:T(8,128)S(1)} collective-permute-done((f32[2,32,8,128]{3,2,1,0:T(8,128)S(1)}, f32[2,32,8,128]{3,2,1,0:T(8,128)S(1)}, u32[]{:S(2)}, u32[]{:S(2)}) %collective-permute-start.1) | collective-permute-done | bytes 262176 | tf_op jit(solution)/shard_map/ppermute | solution.py:186
  122.7 0.9 pad_maximum_fusion.2
  123.6 0.1 pad_maximum_fusion
  123.7 1.8 %fusion.9.x_ref = f32[4,72,256]{2,1,0:T(8,128)} fusion(f32[4,72,1024]{2,1,0:T(8,128)S(1)} %bitcast.66, f32[256,1024,1]{1,0,2:T(8,128)S(1)} %bitcast.68), kind=kOutput, calls=%fused_computation.33 | convolution fusion | flops 905969664 | bytes 2523136 | tf_op jit(solution)/shard_map/dot_general | solution.py:480
  125.6 14.0 %sum_4.1 = f32[4,72,256]{2,1,0:T(8,128)} custom-call(f32[4,72,256]{2,1,0:T(8,128)} %fusion.9.x_ref), custom_call_target="tpu_custom_call" | custom-call | tf_op jit(solution)/shard_map/sum_4/pallas_call | solution.py:170
  139.6 0.8 copy.34
  140.4 34.4 %solve.1 = f32[256,32]{1,0:T(8,128)} custom-call(f32[288,256]{1,0:T(8,128)} %bitcast.71), custom_call_target="tpu_custom_call" | custom-call | flops 40000000 | bytes 60000000 | tf_op jit(solution)/shard_map/solve/pallas_call | solution.py:485
  174.9 0.1 reduce_sum.72
  175.2 0.2 fusion.1
  175.4 0.3 copy.30
  175.8 0.6 copy-done.7
  176.3 1.1 convolution_add_fusion
  177.4 0.7 copy.33
  (39 shorter events, 0.5 us)
Async XLA Ops:
  0.6 112.7 %collective-permute-start = (f32[1,32,8,128]{3,2,1,0:T(8,128)}, f32[1,32,8,128]{3,2,1,0:T(8,128)S(1)}, u32[]{:S(2)}, u32[]{:S(2)}) collective-permute-start(f32[1,32,8,128]{3,2,1,0:T(8,128)} %bitcast.62), channel_id=1, source_target_pairs={{0,16},{4,20},{8,24},{12,28},{16,0},{20,4},{24,8},{28,12},{1,17},{... | collective-permute-start | bytes 393224 | tf_op jit(solution)/shard_map/ppermute | solution.py:186
  82.8 9.9 %copy-start.8 = (f32[32,2,512]{2,1,0:T(2,128)S(1)}, f32[32,2,512]{2,1,0:T(2,128)}, u32[]{:S(2)}) copy-start(f32[32,2,512]{2,1,0:T(2,128)} %param.20) | copy-start | bytes 393220
  82.8 10.0 %copy-start.9 = (f32[2,512]{1,0:T(2,128)S(1)}, f32[2,512]{1,0:T(2,128)}, u32[]{:S(2)}) copy-start(f32[2,512]{1,0:T(2,128)} %param.19) | copy-start | bytes 12292
  82.8 10.0 %copy-start.10 = (f32[2,512]{1,0:T(2,128)S(1)}, f32[2,512]{1,0:T(2,128)}, u32[]{:S(2)}) copy-start(f32[2,512]{1,0:T(2,128)} %param.18) | copy-start | bytes 12292
  92.6 19.1 %copy-start.4 = (f32[64,512]{1,0:T(8,128)}, f32[64,512]{1,0:T(8,128)S(1)}, u32[]{:S(2)}) copy-start(f32[64,512]{1,0:T(8,128)S(1)} %reduce_sum.65) | copy-start | bytes 393220
  111.7 1.5 copy-start
  113.1 0.9 copy-start.1
  114.0 9.5 %copy-start.6 = (f32[32,1024]{1,0:T(8,128)S(1)}, f32[32,1024]{1,0:T(8,128)}, u32[]{:S(2)}) copy-start(f32[32,1024]{1,0:T(8,128)} %get-tuple-element.7) | copy-start | bytes 393220
  114.0 8.6 %collective-permute-start.1 = (f32[2,32,8,128]{3,2,1,0:T(8,128)S(1)}, f32[2,32,8,128]{3,2,1,0:T(8,128)S(1)}, u32[]{:S(2)}, u32[]{:S(2)}) collective-permute-start(f32[2,32,8,128]{3,2,1,0:T(8,128)S(1)} %pad_maximum_fusion.3), channel_id=1, source_target_pairs={{0,8},{4,12},{8,0},{12,4},{16,24},{20,28},{24,16},{28,20},{1,9},{5... | collective-permute-start | bytes 786440 | tf_op jit(solution)/shard_map/ppermute | solution.py:186
  122.7 0.9 copy-start.2
  123.6 51.4 %collective-permute-start.2 = (f32[4,32,8,128]{3,2,1,0:T(8,128)}, f32[4,32,8,128]{3,2,1,0:T(8,128)S(1)}, u32[]{:S(2)}, u32[]{:S(2)}) collective-permute-start(f32[4,32,8,128]{3,2,1,0:T(8,128)} %pad_maximum_fusion.2), channel_id=1, source_target_pairs={{0,4},{4,0},{8,12},{12,8},{16,20},{20,16},{24,28},{28,24},{1,5},{5... | collective-permute-start | bytes 1572872 | tf_op jit(solution)/shard_map/ppermute | solution.py:186
  123.7 15.8 %copy-start.5 = (f32[64,512]{1,0:T(8,128)S(1)}, f32[64,512]{1,0:T(8,128)}, u32[]{:S(2)}) copy-start(f32[64,512]{1,0:T(8,128)} %copy-done.4) | copy-start | bytes 393220
  125.5 49.3 %copy-start.3 = (f32[2,32,8,128]{3,2,1,0:T(8,128)S(1)}, f32[2,32,8,128]{3,2,1,0:T(8,128)}, u32[]{:S(2)}) copy-start(f32[2,32,8,128]{3,2,1,0:T(8,128)} %copy-done.2) | copy-start | bytes 786436
  175.4 0.9 copy-start.7

commit v3 on v2

--- a/solution.py
+++ b/solution.py
@@ -179,18 +179,15 @@
     )(x)
 
 
-def permuted_gather(x, axis):
+def permuted_step(held, axis, bit):
     n = lax.axis_size(axis)
-    held = x[None]
-    for bit in doubling_bits(n):
-        other = lax.ppermute(held, axis, [(i, i ^ bit) for i in range(n)])
-        held = jnp.concatenate([held, other], 0)
-    return held
+    other = lax.ppermute(held, axis, [(i, i ^ bit) for i in range(n)])
+    return jnp.concatenate([held, other], 0)
 
 
 def route_body(
     seg_count, level_count, members, gauges, hours, param_count,
-    basin_ref, ints_ref,
+    basin_ref, down_ref, count_ref, gauge_row_ref, gauge_pack_ref,
     meta_ref, prior_ref, cos_ref, pin_ref, pout_ref, lat_hbm,
     out_ref,
     up_ref, flow_ref, row_ref, now_ref, back_ref, carry_ref, par_ref, raw_ref, ready_ref, sem,
@@ -268,7 +265,7 @@
         def block(j, _):
             here = level * lev + j
             b = seg * seg_blocks + here
-            live = place < ints_ref[seg, 1, here]
+            live = place < count_ref[b]
             now = now_ref[pl.ds(b, 1), :]
             back = back_ref[pl.ds(b, 1), :]
             carry = carry_ref[pl.ds(b, 1), :]
@@ -294,7 +291,7 @@
             up_ref[parity * lev + j] = jnp.zeros((2 * rows, LANES), jnp.float32)
             flow_ref[pl.ds(here * 2 * rows, rows), :] = out0
             flow_ref[pl.ds(here * 2 * rows + rows, rows), :] = out1
-            target = (1 - parity) * lev + ints_ref[seg, 0, here]
+            target = (1 - parity) * lev + down_ref[b]
             up_ref[target, :rows] += out0
             up_ref[target, rows:] += out1
             return 0
@@ -306,10 +303,11 @@
     one_lane = lax.broadcasted_iota(jnp.int32, (1, LANES), 1) // members
 
     def observe(seg):
+        first_gauge = seg * gauges
+
         def one(g, _):
-            slot = ints_ref[seg, 2 + g // LANES, g % LANES]
-            row = (slot // LANES) * (2 * rows) + slot % rows
-            keep = one_lane == (slot % LANES) // rows
+            row = gauge_row_ref[first_gauge + g]
+            keep = one_lane == gauge_pack_ref[first_gauge + g]
             row_ref[pl.ds(g, 1), :] = jnp.where(keep, flow_ref[pl.ds(row, 1), :], 0.0)
             row_ref[pl.ds(gauges + g, 1), :] = jnp.where(
                 keep, flow_ref[pl.ds(row + rows, 1), :], 0.0
@@ -341,25 +339,21 @@
     lax.fori_loop(first + 1, seg_count, later, 0)
 
 
-def invert_small(d):
+def invert_small(d, panel=8):
     size = d.shape[0]
     lane = lax.broadcasted_iota(jnp.int32, d.shape, 1)
     sub = lax.broadcasted_iota(jnp.int32, d.shape, 0)
-    for j in range(0, size, 2):
-        i = j + 1
-        row0, row1 = d[j : j + 1, :], d[i : i + 1, :]
-        col0, col1 = d[:, j : j + 1], d[:, i : i + 1]
-        a, b = d[j : j + 1, j : j + 1], d[j : j + 1, i : i + 1]
-        e, f = d[i : i + 1, j : j + 1], d[i : i + 1, i : i + 1]
-        inv = 1.0 / (a * f - b * e)
-        at0, at1 = lane[:1] == j, lane[:1] == i
-        row0 = jnp.where(at0, 1.0, jnp.where(at1, 0.0, row0))
-        row1 = jnp.where(at0, 0.0, jnp.where(at1, 1.0, row1))
-        new0 = (f * row0 - b * row1) * inv
-        new1 = (a * row1 - e * row0) * inv
-        kept = jnp.where((lane == j) | (lane == i), 0.0, d)
-        rest = kept - (col0 * new0 + col1 * new1)
-        d = jnp.where(sub == j, new0, jnp.where(sub == i, new1, rest))
+    for base in range(0, size, panel):
+        cols = [jnp.broadcast_to(d[:, base + i : base + i + 1], d.shape) for i in range(panel)]
+        for i in range(panel):
+            j = base + i
+            pivot = cols[i]
+            inv = 1.0 / pivot[j : j + 1, :]
+            row = jnp.where(lane[:1] == j, 1.0, d[j : j + 1, :]) * inv
+            d = jnp.where(sub == j, row, jnp.where(lane == j, 0.0, d) - pivot * row)
+            for l in range(i + 1, panel):
+                factor = pivot[base + l : base + l + 1, :] * inv
+                cols[l] = jnp.where(sub == j, factor, cols[l] - pivot * factor)
     return d
 
 
@@ -407,7 +401,8 @@
     packs = LANES // md
     f32 = jnp.float32
 
-    prior_all = permuted_gather(prior_params, "member").reshape(members, param_count * block_dev)
+    prior_steps = doubling_bits(n_member)
+    held = permuted_step(prior_params[None], "member", prior_steps[0])
 
     gauge_rows = gauges // block_dev
     extra = -(md * 2 + 2 + gauge_rows) % 8
@@ -423,7 +418,11 @@
         0,
     )
     meta_all = exchange(meta, "basin", 1)
-    ints_all = meta_all[:, md * 2 : md * 2 + 2 + gauge_rows].astype(jnp.int32)
+    down_all = meta_all[:, md * 2].reshape(-1).astype(jnp.int32)
+    count_all = meta_all[:, md * 2 + 1].reshape(-1).astype(jnp.int32)
+    slots = meta_all[:, md * 2 + 2 : md * 2 + 2 + gauge_rows].reshape(-1).astype(jnp.int32)
+    gauge_row = slots // LANES * (hours * md) + slots % md
+    gauge_pack = slots % LANES // md
 
     modes = param_count - 2
     lane_pos = np.arange(LANES)
@@ -433,13 +432,16 @@
 
     lateral = lateral_flow.reshape(md, hours, block_dev, LANES)
     lateral = jnp.swapaxes(lateral, 1, 2).reshape(md, block_dev * hours, LANES)
+    held, meta_all = lax.optimization_barrier((held, meta_all))
+    for bit in prior_steps[1:-1]:
+        held = permuted_step(held, "member", bit)
     basin_idx = lax.axis_index("basin").astype(jnp.int32).reshape(1)
     seg_coef = VMEM((basins * block_dev, LANES), f32)
 
     parts = pl.pallas_call(
         functools.partial(route_body, basins, level_count, md, gauges, hours, param_count),
         out_shape=jax.ShapeDtypeStruct((basins, 2 * md, gauges), f32),
-        in_specs=[smem_spec()] * 2 + [vmem_spec()] * 5 + [pl.BlockSpec(memory_space=pl.ANY)],
+        in_specs=[smem_spec()] * 5 + [vmem_spec()] * 5 + [pl.BlockSpec(memory_space=pl.ANY)],
         out_specs=vmem_spec(),
         scratch_shapes=[
             VMEM((2 * BLK_LEV, 2 * md, LANES), f32),
@@ -458,9 +460,12 @@
         ),
         name="route",
     )(
-        basin_idx, ints_all, meta_all, prior_params, cosine,
+        basin_idx, down_all, count_all, gauge_row, gauge_pack, meta_all, prior_params, cosine,
         inflow_start.reshape(block_dev, LANES), outflow_start.reshape(block_dev, LANES), lateral,
     )
+    parts, held = lax.optimization_barrier((parts, held))
+    held = permuted_step(held, "member", prior_steps[-1])
+    prior_all = held.reshape(members, param_count * block_dev)
     arrived = exchange(parts, "basin", 2, spread_out=True)
     flows = jnp.sum(arrived, 0)
     pred = inverse_sinh(flows).reshape(hours, md, gauges)

time: 179 us -> 112 us (0.63)
  Pallas kernels: 148 us -> 85.7 us
  waiting for transfers between devices: 8.41 us -> 0.01 us
  starting transfers between devices: 4.2 us -> 6.21 us
    pallas_call x1, Pallas kernels: 65.7 us -> 28.5 us  [shards(): pl.pallas_call(functools.partial(route_body, basins, level_count, md, gau...]
    pallas_call x1, Pallas kernels: 34.4 us -> 12.7 us  [shards(): pl.pallas_call(functools.partial(solve_body, n_member, md), out_shape=jax...]
    ppermute x3, waiting for transfers between devices: 8.41 us -> 0.01 us  [permuted_step(): other = lax.ppermute(held, axis, [(i, i ^ bit) for i in range(n)])]
    ppermute x3, starting transfers between devices: 4.2 us -> 6.21 us  [permuted_step(): other = lax.ppermute(held, axis, [(i, i ^ bit) for i in range(n)])]
    unnamed x28 -> x16, local copies, waits for them, and re-layouts: 3.82 us -> 3.22 us
  transfers between devices with their start and end apart: 3 -> 3, of which waited for: 1 -> 0; matrix products, arithmetic and copies ran while one was open for 7% -> 10% of each run, Pallas kernels for 83% -> 55%
where the time goes in v3:
time: 112 us
  Pallas kernels  85.7 us (77%)
  other arithmetic  9.33 us (8%)
  local copies, waits for them, and re-layouts  6.49 us (6%)
  starting transfers between devices  6.21 us (6%)
  matrix products  2.95 us (3%)
    pallas_call x1, Pallas kernels, shards(): pl.pallas_call(functools.partial(route_body, basins, level_count, md, gau...  28.5 us
    pallas_call x1, Pallas kernels, doubling_gather(): pl.pallas_call(functools.partial(doubling_body, axis, n), out_shape=jax.S...  16.3 us
    pallas_call x2, Pallas kernels, exchange(): pl.pallas_call(functools.partial(exchange_body, axis, n, spread_out), out...  15.2 us
    pallas_call x1, Pallas kernels, sum_over(): pl.pallas_call(functools.partial(sum_body, axis, n), out_shape=jax.ShapeD...  13.1 us
    pallas_call x1, Pallas kernels, shards(): pl.pallas_call(functools.partial(solve_body, n_member, md), out_shape=jax...  12.7 us
    ppermute x3, starting transfers between devices, permuted_step(): other = lax.ppermute(held, axis, [(i, i ^ bit) for i in range(n)])  6.21 us
    unnamed x16, local copies, waits for them, and re-layouts  3.22 us
  transfers between devices with their start and end apart: 3, of which 0 were waited for; matrix products, arithmetic and copies ran while one was open for 10% of the time, Pallas kernels for 55%

profile of v3, /device:TPU:0, one launch (start us, length us, event | category | flops | bytes accessed | tf_op | source)
XLA Modules:
  0.0 111.6 jit_solution(11197559386593282652)
XLA Ops:
  0.6 4.1 %collective-permute-start = (f32[1,32,8,128]{3,2,1,0:T(8,128)}, f32[1,32,8,128]{3,2,1,0:T(8,128)S(1)}, u32[]{:S(2)}, u32[]{:S(2)}) collective-permute-start(f32[1,32,8,128]{3,2,1,0:T(8,128)} %bitcast.70), channel_id=1, source_target_pairs={{0,16},{4,20},{8,24},{12,28},{16,0},{20,4},{24,8},{28,12},{1,17},{... | collective-permute-start | bytes 393224 | tf_op jit(solution)/shard_map/ppermute | solution.py:184
  4.8 1.0 copy.32
  5.8 0.7 convert_bitcast_fusion
  6.4 0.7 convert_bitcast_fusion.1
  7.1 1.8 %concatenate.21.x_ref = f32[72,128]{1,0:T(8,128)} concatenate(f32[32,128]{1,0:T(8,128)S(1)} %get-tuple-element.23, f32[32,128]{1,0:T(8,128)S(1)} %get-tuple-element.22, f32[1,128]{1,0:T(1,128)S(1)} %get-tuple-element.29, f32[1,128]{1,0:T(1,128)S(1)} %get-tuple-element.28, f32[4,128]{1,0:T(4,128)S(1)} %convert_bitcast_fusion, f32[2,128]{1,0:T(2,128)S(1)} %broadcast_in_dim.16), dimensions={0} | concatenate | bytes 73728 | tf_op jit(solution)/shard_map/concatenate | solution.py:409
  8.9 6.8 %exchange_1.1.meta_ref = f32[4,72,128]{2,1,0:T(8,128)} custom-call(f32[72,128]{1,0:T(8,128)} %concatenate.21.x_ref), custom_call_target="tpu_custom_call" | custom-call | tf_op jit(solution)/shard_map/exchange_1/pallas_call | solution.py:61
  15.8 0.7 slice_convert_fusion
  16.5 0.6 add_select_fusion
  17.1 1.1 fusion.15
  18.2 1.4 %slice_convert_fusion.1 = (s32[4,1,128]{2,1,0:T(1,128)}, s32[4,1,128]{2,1,0:T(1,128)}) fusion(f32[4,72,128]{2,1,0:T(8,128)} %exchange_1.1.meta_ref), kind=kLoop, calls=%fused_computation.48 | loop fusion | flops 1024 | bytes 8192 | tf_op jit(solution)/shard_map/convert_element_type | solution.py:422
  19.6 0.9 pad_maximum_fusion.3
  20.5 1.6 %collective-permute-start.1 = (f32[2,32,8,128]{3,2,1,0:T(8,128)S(1)}, f32[2,32,8,128]{3,2,1,0:T(8,128)S(1)}, u32[]{:S(2)}, u32[]{:S(2)}) collective-permute-start(f32[2,32,8,128]{3,2,1,0:T(8,128)S(1)} %pad_maximum_fusion.3), channel_id=1, source_target_pairs={{0,8},{4,12},{8,0},{12,4},{16,24},{20,28},{24,16},{28,20},{1,9},{5... | collective-permute-start | bytes 786440 | tf_op jit(solution)/shard_map/ppermute | solution.py:184
  22.3 28.5 %route.1.x_ref = f32[4,64,512]{2,1,0:T(8,128)} custom-call(s32[1]{0:T(128)} %bitcast.basin_ref, s32[512]{0:T(512)} %bitcast.82, s32[512]{0:T(512)} %bitcast.81, s32[2048]{0:T(1024)} %get-tuple-element.25.gauge_row_ref, s32[2048]{0:T(1024)} %get-tuple-element.24.gauge_pack_ref, f32[4,72,128]{2,1,0:T(8,128)} %exchange_1.1.meta_ref, f32[32,8,128]{2,1,0:T(8,128)} %prior_ref.1, ...), custom_call_target="tpu_custom_call" | custom-call | flops 40000000 | bytes 60000000 | tf_op jit(solution)/shard_map/route/pallas_call | solution.py:441
  50.8 8.3 %exchange_2.1 = f32[4,64,512]{2,1,0:T(8,128)} custom-call(f32[4,64,512]{2,1,0:T(8,128)} %route.1.x_ref), custom_call_target="tpu_custom_call" | custom-call | tf_op jit(solution)/shard_map/exchange_2/pallas_call | solution.py:61
  59.2 1.1 reduce_sum.41
  60.4 0.7 pad_maximum_fusion.4
  61.0 16.3 %doubling_3.1 = f32[8,32,1024]{2,1,0:T(8,128)} custom-call(f32[32,1024]{1,0:T(8,128)} %get-tuple-element.16.x_ref), custom_call_target="tpu_custom_call" | custom-call | tf_op jit(solution)/shard_map/doubling_3/pallas_call | solution.py:112
  77.4 1.4 %reduce_sum.42 = f32[1024]{0:T(1024)S(1)} reduce(f32[8,32,1024]{2,1,0:T(8,128)} %doubling_3.1, f32[]{:T(128)} %constant.57.clone.1), dimensions={0,1}, to_apply=%region_1.2 | reduce | flops 261120 | bytes 1052676 | tf_op jit(solution)/shard_map/reduce_sum | solution.py:480
  78.9 0.2 subtract_divide_fusion
  79.0 0.1 fusion.2
  79.2 0.4 collective-permute-start.2
  79.7 0.1 reduce_sum.43
  79.9 1.8 %fusion.16.x_ref = f32[4,72,256]{2,1,0:T(8,128)} fusion(f32[4,72,1024]{2,1,0:T(8,128)S(1)} %bitcast.65, f32[256,1024,1]{1,0,2:T(8,128)S(1)} %bitcast.67), kind=kOutput, calls=%fused_computation.55 | convolution fusion | flops 905969664 | bytes 2523136 | tf_op jit(solution)/shard_map/dot_general | solution.py:485
  81.7 13.1 %sum_4.1 = f32[4,72,256]{2,1,0:T(8,128)} custom-call(f32[4,72,256]{2,1,0:T(8,128)} %fusion.16.x_ref), custom_call_target="tpu_custom_call" | custom-call | tf_op jit(solution)/shard_map/sum_4/pallas_call | solution.py:170
  94.9 0.8 copy.34
  95.6 12.7 %solve.1 = f32[256,32]{1,0:T(8,128)} custom-call(f32[288,256]{1,0:T(8,128)} %bitcast.72), custom_call_target="tpu_custom_call" | custom-call | flops 40000000 | bytes 60000000 | tf_op jit(solution)/shard_map/solve/pallas_call | solution.py:490
  108.3 0.1 reduce_sum.44
  108.5 0.2 fusion.1
  108.8 0.3 copy.30
  109.2 0.5 copy-done.1
  109.8 1.1 convolution_add_fusion
  110.9 0.7 copy.33
  (27 shorter events, 0.6 us)
Async XLA Ops:
  0.6 21.5 %copy-start.3 = (f32[2,512]{1,0:T(2,128)S(1)}, f32[2,512]{1,0:T(2,128)}, u32[]{:S(2)}) copy-start(f32[2,512]{1,0:T(2,128)} %param.19) | copy-start | bytes 12292
  0.6 21.6 %copy-start.4 = (f32[2,512]{1,0:T(2,128)S(1)}, f32[2,512]{1,0:T(2,128)}, u32[]{:S(2)}) copy-start(f32[2,512]{1,0:T(2,128)} %param.18) | copy-start | bytes 12292
  0.6 19.0 %collective-permute-start = (f32[1,32,8,128]{3,2,1,0:T(8,128)}, f32[1,32,8,128]{3,2,1,0:T(8,128)S(1)}, u32[]{:S(2)}, u32[]{:S(2)}) collective-permute-start(f32[1,32,8,128]{3,2,1,0:T(8,128)} %bitcast.70), channel_id=1, source_target_pairs={{0,16},{4,20},{8,24},{12,28},{16,0},{20,4},{24,8},{28,12},{1,17},{... | collective-permute-start | bytes 393224 | tf_op jit(solution)/shard_map/ppermute | solution.py:184
  20.5 30.2 %collective-permute-start.1 = (f32[2,32,8,128]{3,2,1,0:T(8,128)S(1)}, f32[2,32,8,128]{3,2,1,0:T(8,128)S(1)}, u32[]{:S(2)}, u32[]{:S(2)}) collective-permute-start(f32[2,32,8,128]{3,2,1,0:T(8,128)S(1)} %pad_maximum_fusion.3), channel_id=1, source_target_pairs={{0,8},{4,12},{8,0},{12,4},{16,24},{20,28},{24,16},{28,20},{1,9},{5... | collective-permute-start | bytes 786440 | tf_op jit(solution)/shard_map/ppermute | solution.py:184
  77.3 1.5 %copy-start = (f32[8,32,1024]{2,1,0:T(8,128)S(1)}, f32[8,32,1024]{2,1,0:T(8,128)}, u32[]{:S(2)}) copy-start(f32[8,32,1024]{2,1,0:T(8,128)} %doubling_3.1) | copy-start | bytes 3145732
  79.2 29.1 %collective-permute-start.2 = (f32[4,32,8,128]{3,2,1,0:T(8,128)S(1)}, f32[4,32,8,128]{3,2,1,0:T(8,128)S(1)}, u32[]{:S(2)}, u32[]{:S(2)}) collective-permute-start(f32[4,32,8,128]{3,2,1,0:T(8,128)S(1)} %pad_maximum_fusion.2), channel_id=1, source_target_pairs={{0,4},{4,0},{8,12},{12,8},{16,20},{20,16},{24,28},{28,24},{1,5},{5... | collective-permute-start | bytes 1572872 | tf_op jit(solution)/shard_map/ppermute | solution.py:184
  108.8 0.9 copy-start.1
  108.8 1.0 copy-start.2

commit v4 on v3

--- a/solution.py
+++ b/solution.py
@@ -82,46 +82,79 @@
     return bits
 
 
-def doubling_body(axis, n, x_ref, o_ref, send_sem, recv_sem, own_sem):
-    me = lax.axis_index(axis)
+def observed_body(
+    hours, n_basin, n, x_ref, o_ref, land_ref, part_send, part_recv, send_sem, recv_sem
+):
+    basin = lax.axis_index("basin")
+    me = lax.axis_index("member")
     partners = [me + bit * (1 - 2 * lax.rem(me // bit, 2)) for bit in doubling_bits(n)]
     barrier = pltpu.get_barrier_semaphore()
+    for i in range(1, n_basin):
+        pl.semaphore_signal(
+            barrier, inc=1, device_id={"basin": lax.rem(basin + i, n_basin)}, device_id_type=MESH
+        )
     for partner in partners:
-        pl.semaphore_signal(barrier, inc=1, device_id={axis: partner}, device_id_type=MESH)
-    own = pltpu.make_async_copy(x_ref, o_ref.at[0], own_sem)
-    own.start()
-    own.wait()
-    pl.semaphore_wait(barrier, len(partners))
-    for k, partner in enumerate(partners):
-        held = 2**k
-        copy = pltpu.make_async_remote_copy(
-            src_ref=o_ref.at[pl.ds(0, held)],
-            dst_ref=o_ref.at[pl.ds(held, held)],
-            send_sem=send_sem.at[k],
-            recv_sem=recv_sem.at[k],
-            device_id={axis: partner},
-            device_id_type=MESH,
-        )
+        pl.semaphore_signal(barrier, inc=1, device_id={"member": partner}, device_id_type=MESH)
+    pl.semaphore_wait(barrier, n_basin - 1 + len(partners))
+    parts = []
+    for i in range(1, n_basin):
+        peer = lax.rem(basin + i, n_basin)
+        parts.append(
+            pltpu.make_async_remote_copy(
+                src_ref=x_ref.at[peer], dst_ref=land_ref.at[i - 1],
+                send_sem=part_send.at[i - 1], recv_sem=part_recv.at[i - 1],
+                device_id={"basin": peer}, device_id_type=MESH,
+            )
+        )
+    for copy in parts:
         copy.start()
+    for copy in parts:
         copy.wait()
-
-
-def doubling_gather(x, axis, collective_id):
-    n = lax.axis_size(axis)
-    steps = len(doubling_bits(n))
+    flows = x_ref[basin]
+    for i in range(1, n_basin):
+        flows = flows + land_ref[i - 1]
+    pred = inverse_sinh(flows)
+    rows = o_ref.shape[1]
+    gauges = x_ref.shape[2]
+    for h in range(hours):
+        o_ref[0, :, h * gauges : (h + 1) * gauges] = pred[h * rows : (h + 1) * rows]
+
+    copies = {}
+    for p in range(n):
+        if p:
+            copies[p].wait_recv()
+        for k, partner in enumerate(partners):
+            to = 2**k + p
+            if p < 2**k:
+                copies[to] = pltpu.make_async_remote_copy(
+                    src_ref=o_ref.at[p], dst_ref=o_ref.at[to],
+                    send_sem=send_sem.at[to - 1], recv_sem=recv_sem.at[to - 1],
+                    device_id={"member": partner}, device_id_type=MESH,
+                )
+                copies[to].start()
+    for p in range(1, n):
+        copies[p].wait_send()
+
+
+def observed_gather(parts, hours, collective_id):
+    n = lax.axis_size("member")
+    n_basin = lax.axis_size("basin")
+    rows, gauges = parts.shape[1] // hours, parts.shape[2]
     return pl.pallas_call(
-        functools.partial(doubling_body, axis, n),
-        out_shape=jax.ShapeDtypeStruct((n,) + x.shape, x.dtype),
+        functools.partial(observed_body, hours, n_basin, n),
+        out_shape=jax.ShapeDtypeStruct((n, rows, hours * gauges), parts.dtype),
         in_specs=[vmem_spec()],
         out_specs=vmem_spec(),
         scratch_shapes=[
-            pltpu.SemaphoreType.DMA((steps,)),
-            pltpu.SemaphoreType.DMA((steps,)),
-            pltpu.SemaphoreType.DMA,
+            VMEM((n_basin - 1,) + parts.shape[1:], parts.dtype),
+            pltpu.SemaphoreType.DMA((n_basin - 1,)),
+            pltpu.SemaphoreType.DMA((n_basin - 1,)),
+            pltpu.SemaphoreType.DMA((n - 1,)),
+            pltpu.SemaphoreType.DMA((n - 1,)),
         ],
         compiler_params=pltpu.CompilerParams(collective_id=collective_id, has_side_effects=True),
-        name=f"doubling_{collective_id}",
-    )(x)
+        name=f"observed_{collective_id}",
+    )(parts)
 
 
 def sum_body(axis, n, x_ref, o_ref, land_ref, sem1, sem2, sem3, sem4):
@@ -201,11 +234,16 @@
     lane = lax.broadcasted_iota(jnp.int32, shape, 1)
     place = (lane // members) * members + lax.broadcasted_iota(jnp.int32, shape, 0)
 
-    def fetch(m):
-        return pltpu.make_async_copy(lat_hbm.at[m], raw_ref.at[:, m], sem.at[m])
-
-    for m in range(members):
-        fetch(m).start()
+    chunks = sem.shape[0]
+    chunk_rows = seg_blocks * hours // chunks
+
+    def fetch(c, m):
+        span = pl.ds(c * chunk_rows, chunk_rows)
+        return pltpu.make_async_copy(lat_hbm.at[m, span], raw_ref.at[span, m], sem.at[c, m])
+
+    for c in range(chunks):
+        for m in range(members):
+            fetch(c, m).start()
 
     def clear(i, _):
         up_ref[i] = jnp.zeros((2 * rows, LANES), jnp.float32)
@@ -229,8 +267,6 @@
     lax.fori_loop(first, seg_count, coefficients, 0)
     for k in range(param_count - 2):
         par_ref[k] = turned(0.2 * prior_ref[:, 2 + k, :])
-    for m in range(members):
-        fetch(m).wait()
 
     def place_group(tiles):
         flat = jnp.concatenate(tiles, axis=0).T
@@ -259,7 +295,11 @@
                 ready_ref[base + i, hours + n] = tile
         return 0
 
-    lax.fori_loop(0, seg_blocks // packs, relayout, 0, unroll=2)
+    chunk_groups = seg_blocks // packs // chunks
+    for c in range(chunks):
+        for m in range(members):
+            fetch(c, m).wait()
+        lax.fori_loop(c * chunk_groups, (c + 1) * chunk_groups, relayout, 0, unroll=2)
 
     def sweep(seg, level, parity, own):
         def block(j, _):
@@ -453,7 +493,7 @@
             VMEM((modes, block_dev, LANES), f32),
             VMEM((block_dev * hours, md, LANES), f32),
             VMEM((block_dev, hours + 2, md, LANES), f32),
-            pltpu.SemaphoreType.DMA((md,)),
+            pltpu.SemaphoreType.DMA((4, md)),
         ],
         cost_estimate=pl.CostEstimate(
             flops=40_000_000, bytes_accessed=60_000_000, transcendentals=0
@@ -466,12 +506,10 @@
     parts, held = lax.optimization_barrier((parts, held))
     held = permuted_step(held, "member", prior_steps[-1])
     prior_all = held.reshape(members, param_count * block_dev)
-    arrived = exchange(parts, "basin", 2, spread_out=True)
-    flows = jnp.sum(arrived, 0)
-    pred = inverse_sinh(flows).reshape(hours, md, gauges)
-    predicted = jnp.swapaxes(pred, 0, 1)
-    flat = jnp.concatenate([pred[h] for h in range(hours)], axis=1)
-    pred_all = doubling_gather(flat, "member", 3).reshape(members, hours * gauges)
+    gathered = observed_gather(parts, hours, 2)
+    flat = gathered[0]
+    predicted = flat.reshape(md, hours, gauges)
+    pred_all = gathered.reshape(members, hours * gauges)
 
     spread = jnp.sqrt(obs_var).reshape(1, -1)
     spread_root = math.sqrt(members - 1.0)

time: 112 us -> 109 us (0.973)
  other arithmetic: 9.33 us -> 7.49 us
  Pallas kernels: 85.7 us -> 84.4 us
    pallas_call x2 -> x1, Pallas kernels: 15.2 us -> 6.82 us  [exchange(): pl.pallas_call(functools.partial(exchange_body, axis, n, spread_out), out...]
    pallas_call x1, Pallas kernels: 16.3 us -> 21.4 us  [observed_gather(): pl.pallas_call(functools.partial(observed_body, hours, n_basin, n), out_s...]
    pallas_call x1, Pallas kernels: 13.1 us -> 14.9 us  [sum_over(): pl.pallas_call(functools.partial(sum_body, axis, n), out_shape=jax.ShapeD...]
    unnamed x16 -> x15, local copies, waits for them, and re-layouts: 3.22 us -> 2.47 us
  transfers between devices with their start and end apart: 3 -> 3, of which waited for: 0 -> 0; matrix products, arithmetic and copies ran while one was open for 10% -> 12% of each run, Pallas kernels for 55% -> 78%
where the time goes in v4:
time: 109 us; the launch traced here: 108 us
  Pallas kernels  84.4 us (77%)
  other arithmetic  7.49 us (7%)
  local copies, waits for them, and re-layouts  6.49 us (6%)
  starting transfers between devices  5.84 us (5%)
  matrix products  2.97 us (3%)
    pallas_call x1, Pallas kernels, shards(): pl.pallas_call(functools.partial(route_body, basins, level_count, md, gau...  28.7 us
    pallas_call x1, Pallas kernels, observed_gather(): pl.pallas_call(functools.partial(observed_body, hours, n_basin, n), out_s...  21.4 us
    pallas_call x1, Pallas kernels, sum_over(): pl.pallas_call(functools.partial(sum_body, axis, n), out_shape=jax.ShapeD...  14.9 us
    pallas_call x1, Pallas kernels, shards(): pl.pallas_call(functools.partial(solve_body, n_member, md), out_shape=jax...  12.7 us
    pallas_call x1, Pallas kernels, exchange(): pl.pallas_call(functools.partial(exchange_body, axis, n, spread_out), out...  6.82 us
    ppermute x3, starting transfers between devices, permuted_step(): other = lax.ppermute(held, axis, [(i, i ^ bit) for i in range(n)])  5.84 us
    unnamed x15, local copies, waits for them, and re-layouts  2.47 us
  transfers between devices with their start and end apart: 3, of which 0 were waited for; matrix products, arithmetic and copies ran while one was open for 12% of the time, Pallas kernels for 78%

profile of v4, /device:TPU:0, one launch (start us, length us, event | category | flops | bytes accessed | tf_op | source)
XLA Modules:
  0.0 108.1 jit_solution(14687730031569749637)
XLA Ops:
  0.6 4.1 %collective-permute-start = (f32[1,32,8,128]{3,2,1,0:T(8,128)}, f32[1,32,8,128]{3,2,1,0:T(8,128)S(1)}, u32[]{:S(2)}, u32[]{:S(2)}) collective-permute-start(f32[1,32,8,128]{3,2,1,0:T(8,128)} %bitcast.69), channel_id=1, source_target_pairs={{0,16},{4,20},{8,24},{12,28},{16,0},{20,4},{24,8},{28,12},{1,17},{... | collective-permute-start | bytes 393224 | tf_op jit(solution)/shard_map/ppermute | solution.py:217
  4.8 1.0 copy.20
  5.8 0.7 convert_bitcast_fusion
  6.4 0.7 convert_bitcast_fusion.1
  7.1 1.8 %concatenate.18.x_ref = f32[72,128]{1,0:T(8,128)} concatenate(f32[32,128]{1,0:T(8,128)S(1)} %get-tuple-element.17, f32[32,128]{1,0:T(8,128)S(1)} %get-tuple-element.16, f32[1,128]{1,0:T(1,128)S(1)} %get-tuple-element.23, f32[1,128]{1,0:T(1,128)S(1)} %get-tuple-element.22, f32[4,128]{1,0:T(4,128)S(1)} %convert_bitcast_fusion, f32[2,128]{1,0:T(2,128)S(1)} %broadcast_in_dim.16), dimensions={0} | concatenate | bytes 73728 | tf_op jit(solution)/shard_map/concatenate | solution.py:449
  8.9 6.8 %exchange_1.1.meta_ref = f32[4,72,128]{2,1,0:T(8,128)} custom-call(f32[72,128]{1,0:T(8,128)} %concatenate.18.x_ref), custom_call_target="tpu_custom_call" | custom-call | tf_op jit(solution)/shard_map/exchange_1/pallas_call | solution.py:61
  15.8 0.7 slice_convert_fusion
  16.5 0.6 add_select_fusion
  17.1 1.1 %fusion.14 = (f32[32,1,512]{2,1,0:T(1,128)S(1)}, f32[32,1,512]{2,1,0:T(1,128)S(1)}) fusion(f32[32,2,512]{2,1,0:T(2,128)} %param.20), kind=kLoop, calls=%fused_computation.50 | loop fusion | bytes 262144 | tf_op jit(solution)/shard_map/slice | solution.py:516
  18.2 1.4 %slice_convert_fusion.1 = (s32[4,1,128]{2,1,0:T(1,128)}, s32[4,1,128]{2,1,0:T(1,128)}) fusion(f32[4,72,128]{2,1,0:T(8,128)} %exchange_1.1.meta_ref), kind=kLoop, calls=%fused_computation.45 | loop fusion | flops 1024 | bytes 8192 | tf_op jit(solution)/shard_map/convert_element_type | solution.py:462
  19.6 0.9 pad_maximum_fusion.3
  20.5 1.6 %collective-permute-start.1 = (f32[2,32,8,128]{3,2,1,0:T(8,128)S(1)}, f32[2,32,8,128]{3,2,1,0:T(8,128)S(1)}, u32[]{:S(2)}, u32[]{:S(2)}) collective-permute-start(f32[2,32,8,128]{3,2,1,0:T(8,128)S(1)} %pad_maximum_fusion.3), channel_id=1, source_target_pairs={{0,8},{4,12},{8,0},{12,4},{16,24},{20,28},{24,16},{28,20},{1,9},{5... | collective-permute-start | bytes 786440 | tf_op jit(solution)/shard_map/ppermute | solution.py:217
  22.3 28.7 %route.1.x_ref = f32[4,64,512]{2,1,0:T(8,128)} custom-call(s32[1]{0:T(128)} %bitcast.basin_ref, s32[512]{0:T(512)} %bitcast.80, s32[512]{0:T(512)} %bitcast.79, s32[2048]{0:T(1024)} %get-tuple-element.19.gauge_row_ref, s32[2048]{0:T(1024)} %get-tuple-element.18.gauge_pack_ref, f32[4,72,128]{2,1,0:T(8,128)} %exchange_1.1.meta_ref, f32[32,8,128]{2,1,0:T(8,128)} %prior_ref.1, ...), custom_call_target="tpu_custom_call" | custom-call | flops 40000000 | bytes 60000000 | tf_op jit(solution)/shard_map/route/pallas_call | solution.py:481
  51.0 0.1 collective-permute-start.2
  51.1 0.1 reduce_sum.31
  51.2 21.4 %observed_2.1 = f32[8,32,1024]{2,1,0:T(8,128)} custom-call(f32[4,64,512]{2,1,0:T(8,128)} %route.1.x_ref), custom_call_target="tpu_custom_call" | custom-call | tf_op jit(solution)/shard_map/observed_2/pallas_call | solution.py:143
  72.6 1.4 %reduce_sum.30 = f32[1024]{0:T(1024)S(1)} reduce(f32[8,32,1024]{2,1,0:T(8,128)} %observed_2.1, f32[]{:T(128)} %constant.56.clone.1), dimensions={0,1}, to_apply=%region_0.1 | reduce | flops 261120 | bytes 1052676 | tf_op jit(solution)/shard_map/reduce_sum | solution.py:518
  74.0 0.1 copy-done
  74.1 0.1 fusion.2
  74.3 0.1 pad_maximum_fusion
  74.4 0.1 subtract_divide_fusion
  74.6 1.9 %fusion.15.x_ref = f32[4,72,256]{2,1,0:T(8,128)} fusion(f32[4,72,1024]{2,1,0:T(8,128)S(1)} %bitcast.64, f32[256,1024,1]{1,0,2:T(8,128)S(1)} %bitcast.66), kind=kOutput, calls=%fused_computation.51 | convolution fusion | flops 905969664 | bytes 2523136 | tf_op jit(solution)/shard_map/dot_general | solution.py:523
  76.4 14.9 %sum_4.1 = f32[4,72,256]{2,1,0:T(8,128)} custom-call(f32[4,72,256]{2,1,0:T(8,128)} %fusion.15.x_ref), custom_call_target="tpu_custom_call" | custom-call | tf_op jit(solution)/shard_map/sum_4/pallas_call | solution.py:203
  91.4 0.8 reshape_squeeze.2
  92.2 12.7 %solve.1 = f32[256,32]{1,0:T(8,128)} custom-call(f32[288,256]{1,0:T(8,128)} %bitcast.71), custom_call_target="tpu_custom_call" | custom-call | flops 40000000 | bytes 60000000 | tf_op jit(solution)/shard_map/solve/pallas_call | solution.py:528
  104.8 0.1 reduce_sum.32
  105.0 0.1 pad_maximum_fusion.1
  105.1 0.2 fusion.1
  105.3 0.3 copy.18
  105.7 0.5 copy-done.1
  106.3 1.1 %convolution_add_fusion = f32[32,8,128]{2,0,1:T(8,128)S(1)} fusion(f32[8,128,256]{2,1,0:T(8,128)S(1)} %bitcast.68, f32[256,32]{1,0:T(8,128)S(1)} %copy-done.2, f32[32,8,128]{2,1,0:T(8,128)S(1)} %copy-done.1), kind=kOutput, calls=%fused_computation.1 | convolution fusion | flops 100696064 | bytes 1343488 | tf_op jit(solution)/shard_map/dot_general | solution.py:542
  107.4 0.7 copy.21
  (24 shorter events, 0.2 us)
Async XLA Ops:
  0.6 21.5 %copy-start.3 = (f32[2,512]{1,0:T(2,128)S(1)}, f32[2,512]{1,0:T(2,128)}, u32[]{:S(2)}) copy-start(f32[2,512]{1,0:T(2,128)} %param.19) | copy-start | bytes 12292
  0.6 21.6 %copy-start.4 = (f32[2,512]{1,0:T(2,128)S(1)}, f32[2,512]{1,0:T(2,128)}, u32[]{:S(2)}) copy-start(f32[2,512]{1,0:T(2,128)} %param.18) | copy-start | bytes 12292
  0.6 19.0 %collective-permute-start = (f32[1,32,8,128]{3,2,1,0:T(8,128)}, f32[1,32,8,128]{3,2,1,0:T(8,128)S(1)}, u32[]{:S(2)}, u32[]{:S(2)}) collective-permute-start(f32[1,32,8,128]{3,2,1,0:T(8,128)} %bitcast.69), channel_id=1, source_target_pairs={{0,16},{4,20},{8,24},{12,28},{16,0},{20,4},{24,8},{28,12},{1,17},{... | collective-permute-start | bytes 393224 | tf_op jit(solution)/shard_map/ppermute | solution.py:217
  20.5 30.4 %collective-permute-start.1 = (f32[2,32,8,128]{3,2,1,0:T(8,128)S(1)}, f32[2,32,8,128]{3,2,1,0:T(8,128)S(1)}, u32[]{:S(2)}, u32[]{:S(2)}) collective-permute-start(f32[2,32,8,128]{3,2,1,0:T(8,128)S(1)} %pad_maximum_fusion.3), channel_id=1, source_target_pairs={{0,8},{4,12},{8,0},{12,4},{16,24},{20,28},{24,16},{28,20},{1,9},{5... | collective-permute-start | bytes 786440 | tf_op jit(solution)/shard_map/ppermute | solution.py:217
  51.0 53.9 %collective-permute-start.2 = (f32[4,32,8,128]{3,2,1,0:T(8,128)S(1)}, f32[4,32,8,128]{3,2,1,0:T(8,128)S(1)}, u32[]{:S(2)}, u32[]{:S(2)}) collective-permute-start(f32[4,32,8,128]{3,2,1,0:T(8,128)S(1)} %pad_maximum_fusion.2), channel_id=1, source_target_pairs={{0,4},{4,0},{8,12},{12,8},{16,20},{20,16},{24,28},{28,24},{1,5},{5... | collective-permute-start | bytes 1572872 | tf_op jit(solution)/shard_map/ppermute | solution.py:217
  72.6 1.5 %copy-start = (f32[8,32,1024]{2,1,0:T(8,128)S(1)}, f32[8,32,1024]{2,1,0:T(8,128)}, u32[]{:S(2)}) copy-start(f32[8,32,1024]{2,1,0:T(8,128)} %observed_2.1) | copy-start | bytes 3145732
  74.6 16.8 %slice-start = ((f32[8,32,1024]{2,1,0:T(8,128)}), f32[1,32,1024]{2,1,0:T(8,128)S(1)}, s32[]{:S(2)}) async-start(f32[8,32,1024]{2,1,0:T(8,128)} %observed_2.1), calls=%async_computation | async-start | bytes 262144 | tf_op jit(solution)/shard_map/slice | solution.py:510
  105.3 0.9 copy-start.1
  105.3 1.0 copy-start.2
